TPU v7x, 32 devices: a whole 2x2x4 slice. The times are simulated.
32 devices in a mesh: expert: 8 (over z, x), dp: 4 (over y, core).
Axes of the slice: x: 2, y: 2, z: 4, core: 2. Of those that a mesh axis runs over, the one named last changes fastest.
Arguments:
- layer_in: bfloat16 [4096, 1024], P(('expert', 'dp')), may hold values from -6 to 6
- routes: int32 [4096, 2], P(('expert', 'dp')), may hold values from 0 to 15, as said below
- queue_slots: int32 [4096, 2], P(('expert', 'dp')), may hold values from -1 to 4, as said below
- norm_attn: float32 [1024], replicated, may hold values from 0.5 to 1.5
- w_query: bfloat16 [1024, 1024], replicated, may hold values from -0.078125 to 0.078125
- w_key: bfloat16 [1024, 1024], replicated, may hold values from -0.078125 to 0.078125
- w_value: bfloat16 [1024, 1024], replicated, may hold values from -0.1875 to 0.1875
- w_out: bfloat16 [1024, 1024], replicated, may hold values from -0.75 to 0.75
- rel_table: float32 [32, 16], replicated, may hold values from -4 to 4
- norm_moe: float32 [1024], replicated, may hold values from 0.5 to 1.5
- router: float32 [1024, 16], replicated, may hold values from -0.375 to 0.375
- w_gate: bfloat16 [16, 1024, 2816], P('expert', None, 'dp'), may hold values from -0.1875 to 0.1875
- w_up: bfloat16 [16, 1024, 2816], P('expert', None, 'dp'), may hold values from -0.1875 to 0.1875
- w_down: bfloat16 [16, 2816, 1024], P('expert', 'dp'), may hold values from -0.109375 to 0.109375
- cotangent: bfloat16 [4096, 1024], P(('expert', 'dp')), may hold values from -6 to 6
Outputs:
- layer_out: bfloat16 [4096, 1024], P(('expert', 'dp'))
- grad_input: float32 [4096, 1024], P(('expert', 'dp'))
- grad_norm_attn: float32 [1024], replicated
- grad_w_query: float32 [1024, 1024], replicated
- grad_w_key: float32 [1024, 1024], replicated
- grad_w_value: float32 [1024, 1024], replicated
- grad_w_out: float32 [1024, 1024], replicated
- grad_rel_table: float32 [32, 16], replicated
- grad_norm_moe: float32 [1024], replicated
- grad_router: float32 [1024, 16], replicated
- grad_w_gate: float32 [16, 1024, 2816], P('expert', None, 'dp')
- grad_w_up: float32 [16, 1024, 2816], P('expert', None, 'dp')
- grad_w_down: float32 [16, 2816, 1024], P('expert', 'dp')
Inputs may be any that keep to these rules, and one draw needn't show every extreme that they name: `routes`: each token names two different experts. `queue_slots`: A choice's place in its expert's queue within its routing group of 32 consecutive tokens, where all first choices queue before all second choices; -1 where 5 places are already taken. Within a group each place of an expert is held by at most one choice, and an expert's places are taken from 0 upward without gaps.
All inputs are finite; a program needn't handle non-finite values.
Results may differ from a plain program's by a relative error of at most 0.014.
The roundings to bfloat16 on the way count: a program that leaves them out, or rounds other values in their place, can miss the bound.
Values may be sent and summed in bfloat16 or wider, within the bound.
A program may use at most 192 MiB of HBM per device.

v0:
```python
import functools
import math

import jax
import jax.numpy as jnp
from jax import lax
from jax.experimental import pallas as pl
from jax.experimental.pallas import tpu as pltpu
from jax.sharding import PartitionSpec as P

MICRO = 4

epsilon = 1e-06
bucket_edges = (12, 16, 23, 32, 46, 64, 91)
highest = lax.Precision.HIGHEST

MESH = pl.DeviceIdType.MESH
VMEM = pl.BlockSpec(memory_space=pltpu.VMEM)
DMA = pltpu.SemaphoreType.DMA


class Place:
    def __init__(self, n_expert, n_dp):
        self.n_expert, self.n_dp = n_expert, n_dp
        self.nz = math.gcd(n_expert, 4)
        self.nx = n_expert // self.nz
        self.ny = n_dp // 2
        self.e = lax.axis_index("expert")
        self.d = lax.axis_index("dp")
        self.z, self.x = self.e // self.nx, self.e % self.nx
        self.y, self.c = self.d // 2, self.d % 2

    def at(self, z=None, x=None, y=None, c=None, e=None):
        z = self.z if z is None else z
        x = self.x if x is None else x
        y = self.y if y is None else y
        c = self.c if c is None else c
        e = z * self.nx + x if e is None else e
        return (e, y * 2 + c)


def remote(src, dst, send, recv, device):
    copy = pltpu.make_async_remote_copy(
        src_ref=src, dst_ref=dst, send_sem=send, recv_sem=recv, device_id=device, device_id_type=MESH
    )
    copy.start()
    return copy


def greet(devices):
    barrier = pltpu.get_barrier_semaphore()
    for device in devices:
        pl.semaphore_signal(barrier, inc=1, device_id=device, device_id_type=MESH)
    pl.semaphore_wait(barrier, len(devices))


def column_peers(me):
    out = [me.at(c=1 - me.c)]
    out += [me.at(y=(me.y + k) % me.ny) for k in range(1, me.ny)]
    out += [me.at(e=(me.e + k) % me.n_expert) for k in range(1, me.n_expert)]
    return out


class Spread:
    def __init__(self, me, rows, recv, sems):
        self.me, self.rows, self.recv = me, rows, recv
        self.se, self.re, self.sy, self.ry, self.sc, self.rc = sems
        self.came, self.along, self.crossed = {}, {}, {}

    def send(self):
        me = self.me
        for k in range(1, me.n_expert):
            to = (me.e + k) % me.n_expert
            self.came[k] = remote(
                self.rows.at[to], self.recv.at[me.c, me.y * me.n_expert + me.e],
                self.se.at[k], self.re.at[k], me.at(e=to),
            )
        self.recv[me.c, me.y * me.n_expert + me.e] = self.rows[me.e]

    def pass_on(self, blocks):
        me = self.me
        for k in blocks:
            if k:
                self.came[k].wait_recv()
            src = (me.e - k + me.n_expert) % me.n_expert
            block = self.recv.at[me.c, me.y * me.n_expert + src]
            for s in range(1, me.ny):
                self.along[s, k] = remote(
                    block, block, self.sy.at[s - 1, k], self.ry.at[s - 1, k], me.at(y=(me.y + s) % me.ny)
                )

    def pass_column(self):
        me = self.me
        for k in range(1, me.n_expert):
            self.came[k].wait_recv()
        block = self.recv.at[me.c, pl.ds(me.y * me.n_expert, me.n_expert)]
        for s in range(1, me.ny):
            self.along[s, 0] = remote(
                block, block, self.sy.at[s - 1, 0], self.ry.at[s - 1, 0], me.at(y=(me.y + s) % me.ny)
            )

    def cross(self, s):
        me = self.me
        if s:
            for key, copy in self.along.items():
                if key[0] == s:
                    copy.wait_recv()
        block = self.recv.at[me.c, pl.ds((me.y - s + me.ny) % me.ny * me.n_expert, me.n_expert)]
        self.crossed[s] = remote(block, block, self.sc.at[s], self.rc.at[s], me.at(c=1 - me.c))

    def arrive(self):
        for copy in self.crossed.values():
            copy.wait_recv()

    def close(self):
        for copies in (self.came, self.along, self.crossed):
            for copy in copies.values():
                copy.wait_send()


def spread_sems(sizes):
    n_expert, ny = sizes[0], sizes[1] // 2
    most = max(ny - 1, 1)
    return [
        DMA((3, n_expert)), DMA((3, n_expert)), DMA((3, most, n_expert)), DMA((3, most, n_expert)),
        DMA((3, ny)), DMA((3, ny)),
    ]


class Rows:
    def __init__(self, me, rows_per, info_all, gates, tok, send, recv):
        self.me, self.rows_per, self.info_all, self.gates, self.tok = me, rows_per, info_all, gates, tok
        self.send, self.recv, self.copies = send, recv, {}
        self.seq = tok.shape[2]

    def share(self, i, ref):
        block = ref.at[self.me.c]
        mate = self.me.at(c=1 - self.me.c)
        self.copies[i] = remote(block, block, self.send.at[i], self.recv.at[i], mate)

    def hots(self):
        me, seq = self.me, self.seq
        micro, cap, per_core = self.rows_per
        self.copies["info"].wait_recv()
        row_ids = lax.broadcasted_iota(jnp.int32, (me.n_expert * 2 * per_core, seq), 0)
        group = lax.broadcasted_iota(jnp.int32, (1, seq), 1) // (seq // micro)
        self.each = []
        for cc in range(2):
            for k in range(2):
                route = self.info_all[cc, k : k + 1, :]
                slot = self.info_all[cc, 2 + k : 3 + k, :]
                target = (route // 2) * (2 * per_core) + cc * per_core + group * cap + slot
                target = jnp.where((slot >= 0) & (route % 2 == me.c), target, -1)
                self.each.append(jnp.where(row_ids == target, 1.0, 0.0))
        self.both = [(self.each[2 * cc] + self.each[2 * cc + 1]).astype(jnp.bfloat16) for cc in range(2)]

    def gather(self, i):
        self.copies[i].wait_recv()
        total = None
        for cc in range(2):
            term = jnp.dot(self.both[cc], self.tok[i, cc], preferred_element_type=jnp.float32)
            total = term if total is None else total + term
        return total.astype(jnp.bfloat16).reshape(self.me.n_expert, 2 * self.rows_per[2], -1)

    def weights(self):
        self.copies["gates"].wait_recv()
        size = 2 * self.rows_per[2]
        column = None
        for n, hot in enumerate(self.each):
            term = jnp.sum(hot * self.gates[n // 2, n % 2 : n % 2 + 1, :], axis=1, keepdims=True)
            column = term if column is None else column + term
        lane = lax.broadcasted_iota(jnp.int32, (size, 128), 1)
        row = lax.broadcasted_iota(jnp.int32, (size, 128), 0)
        tiles = []
        for e in range(self.me.n_expert):
            block = jnp.where(lane == row, column[e * size : (e + 1) * size, :], 0.0)
            tiles.append(jnp.broadcast_to(jnp.sum(block, axis=0, keepdims=True), (8, 128)))
        return tiles

    def close(self):
        for copy in self.copies.values():
            copy.wait_send()


NAMED = ("info", "gates", 0, 1)


class Named:
    def __init__(self, sems):
        self.at = {name: sems.at[i] for i, name in enumerate(NAMED)}


def rows_scratch(sizes, per_core, seq, width):
    mine = (sizes[0], 2 * per_core, width)
    bf = jnp.bfloat16
    return [
        pltpu.VMEM((2, 8, seq), jnp.int32),
        pltpu.VMEM((2, 8, seq), jnp.float32),
        pltpu.VMEM((2, 2, seq, width), bf),
        DMA((4,)),
        DMA((4,)),
        pltpu.VMEM(mine, bf),
        pltpu.VMEM((sizes[0], 8, 128), jnp.float32),
        pltpu.VMEM(mine, bf),
    ]


def rows_of(me, rows_per, scratch):
    info_all, gates, tok, send, recv = scratch[:5]
    return Rows(me, rows_per, info_all, gates, tok, Named(send), Named(recv))


def spread_kernel(sizes, rows_per, info_ref, moe_ref, cot_ref, w_ref, x_out, w_out, g_out, *scratch):
    me = Place(*sizes)
    c = me.c
    greet(column_peers(me))
    scratch, sems = scratch[:8], scratch[8:]
    rows = rows_of(me, rows_per, scratch)
    info_all, gates, tok = scratch[:3]
    info_all[c] = info_ref[...]
    rows.share("info", info_all)
    gates[c] = w_ref[...]
    rows.share("gates", gates)
    for i, ref in enumerate((moe_ref, cot_ref)):
        tok[i, c] = ref[...]
        rows.share(i, tok.at[i])
    rows.hots()
    buf_x, buf_w, buf_g = scratch[5:]
    out_x, out_w, out_g = [
        Spread(me, buf, recv, [s.at[i] for s in sems])
        for i, (buf, recv) in enumerate(((buf_x, x_out), (buf_w, w_out), (buf_g, g_out)))
    ]
    for i, payload in enumerate((out_x, out_g)):
        payload.rows[...] = rows.gather(i)
        payload.send()
    for e, tile in enumerate(rows.weights()):
        buf_w[e] = tile
    out_w.send()
    for payload in (out_x, out_g):
        payload.pass_on(range(me.n_expert))
        payload.cross(0)
    out_w.pass_column()
    out_w.cross(0)
    for payload in (out_x, out_g, out_w):
        for s in range(1, me.ny):
            payload.cross(s)
    for payload in (out_x, out_g, out_w):
        payload.arrive()
        payload.close()
    rows.close()


def spread(sizes, micro, cap, info, moe, cot, weights):
    n_expert, ny, per_core = sizes[0], sizes[1] // 2, micro * cap
    seq, width = cot.shape
    block = (2, ny * n_expert, 2 * per_core)
    bf = jnp.bfloat16
    return pl.pallas_call(
        functools.partial(spread_kernel, sizes, (micro, cap, per_core)),
        out_shape=(
            jax.ShapeDtypeStruct(block + (width,), bf),
            jax.ShapeDtypeStruct(block[:2] + (8, 128), jnp.float32),
            jax.ShapeDtypeStruct(block + (width,), bf),
        ),
        in_specs=[VMEM] * 4,
        out_specs=(VMEM,) * 3,
        scratch_shapes=rows_scratch(sizes, per_core, seq, width) + spread_sems(sizes),
        name="spread",
        compiler_params=pltpu.CompilerParams(
            collective_id=1, has_side_effects=True, vmem_limit_bytes=48 << 20
        ),
    )(info, moe, cot, weights)


class Back:
    def __init__(self, me, away, own, q_out, r1, stage, r2, final, sems):
        self.me, self.away, self.own = me, away, own
        self.q_out, self.r1, self.stage, self.r2, self.final = q_out, r1, stage, r2, final
        self.sems = sems
        self.ys = [(me.y + k) % me.ny for k in range(me.ny)]
        self.order = list(range(1, me.n_expert)) + [0]
        self.first, self.second, self.third, self.fourth = {}, {}, {}, {}
        self.arrived = set()

    def to_mate(self, i, k):
        me = self.me
        column = pl.ds(self.ys[k] * me.n_expert, me.n_expert)
        self.first[i, k] = remote(
            self.away(i).at[column], self.r1.at[i, column], self.sems[0].at[i, k], self.sems[1].at[i, k],
            me.at(c=1 - me.c),
        )

    def partial(self, i, y, e):
        block = y * self.me.n_expert + e
        return self.own(i, block) + self.r1[i, block].astype(jnp.float32)

    def along_y(self, i):
        me = self.me
        for k in range(1, me.ny):
            self.first[i, k].wait_recv()
            for j in self.order:
                e = (me.e + j) % me.n_expert
                self.stage[i, k - 1, e] = self.partial(i, self.ys[k], e).astype(jnp.bfloat16)
                self.second[i, k, j] = remote(
                    self.stage.at[i, k - 1, e], self.r2.at[i, k - 1, e],
                    self.sems[2].at[i, k - 1, j], self.sems[3].at[i, k - 1, j], me.at(y=self.ys[k]),
                )

    def finish(self, i, order):
        me = self.me
        if (i, 0) not in self.arrived:
            self.arrived.add((i, 0))
            self.first[i, 0].wait_recv()
        for j in order:
            e = (me.e + j) % me.n_expert
            total = self.partial(i, me.y, e)
            for k in range(1, me.ny):
                self.second[i, k, j].wait_recv()
                total = total + self.r2[i, k - 1, e].astype(jnp.float32)
            if j:
                self.final[i, e] = total.astype(jnp.bfloat16)
                self.third[i, j] = remote(
                    self.final.at[i, e], self.q_out.at[i, me.c, me.e],
                    self.sems[4].at[i, j], self.sems[5].at[i, j], me.at(e=e),
                )
            else:
                self.q_out[i, me.c, me.e] = total.astype(jnp.bfloat16)

    def across(self, i):
        for j in self.order[:-1]:
            self.third[i, j].wait_recv()
        block = self.q_out.at[i, self.me.c]
        s, r = self.sems[6].at[i], self.sems[7].at[i]
        self.fourth[i] = remote(block, block, s, r, self.me.at(c=1 - self.me.c))

    def close(self):
        for copy in self.fourth.values():
            copy.wait()
        for copies in (self.first, self.second, self.third):
            for copy in copies.values():
                copy.wait_send()


def back_scratch(sizes, size, width):
    n_expert, ny = sizes[0], sizes[1] // 2
    most = max(ny - 1, 1)
    bf = jnp.bfloat16
    return [
        pltpu.VMEM((2, ny * n_expert, size, width), bf),
        pltpu.VMEM((2, most, n_expert, size, width), bf),
        pltpu.VMEM((2, most, n_expert, size, width), bf),
        pltpu.VMEM((2, n_expert, size, width), bf),
        DMA((2, ny)),
        DMA((2, ny)),
        DMA((2, most, n_expert)),
        DMA((2, most, n_expert)),
        DMA((2, n_expert)),
        DMA((2, n_expert)),
        DMA((2,)),
        DMA((2,)),
    ]


def gather_back_kernel(sizes, p0_ref, p1_ref, q_out, *scratch):
    me = Place(*sizes)
    greet(column_peers(me))
    p_refs = (p0_ref, p1_ref)
    back = Back(
        me, lambda i: p_refs[i].at[1 - me.c],
        lambda i, block: p_refs[i][me.c, block].astype(jnp.float32), q_out, *scratch[:4], scratch[4:],
    )
    for i in range(2):
        for k in reversed(range(me.ny)):
            back.to_mate(i, k)
    for i in range(2):
        back.along_y(i)
    for i in range(2):
        back.finish(i, back.order)
        back.across(i)
    back.close()


def gather_back(sizes, first, second):
    n_expert = sizes[0]
    _, _, size, width = first.shape
    return pl.pallas_call(
        functools.partial(gather_back_kernel, sizes),
        out_shape=jax.ShapeDtypeStruct((2, 2, n_expert, size, width), jnp.bfloat16),
        in_specs=[VMEM] * 2,
        out_specs=VMEM,
        scratch_shapes=back_scratch(sizes, size, width),
        name="gather_back",
        compiler_params=pltpu.CompilerParams(
            collective_id=2, has_side_effects=True, vmem_limit_bytes=48 << 20
        ),
    )(first, second)


def gated_terms(gate_pre, up_pre):
    root = math.sqrt(2.0 / math.pi)
    square = gate_pre * gate_pre
    bend = jnp.tanh(root * (gate_pre + 0.044715 * square * gate_pre))
    half = 0.5 * (1.0 + bend)
    active = gate_pre * half
    slope = half + 0.5 * gate_pre * (1.0 - bend * bend) * root * (1.0 + 3 * 0.044715 * square)
    return active * up_pre, active, up_pre * slope


def bucket_of(relative):
    distance = jnp.abs(relative)
    far_bucket = jnp.full_like(distance, 8)
    for threshold in bucket_edges:
        far_bucket = far_bucket + (distance >= threshold).astype(jnp.int32)
    return jnp.where(distance < 8, distance, far_bucket) + 16 * (relative > 0).astype(jnp.int32)


def row_scale(values):
    return lax.rsqrt(jnp.mean(values * values, axis=-1, keepdims=True) + epsilon)


def dot_as(left, right, contract):
    return lax.dot_general(left, right, (contract, ((), ())), preferred_element_type=jnp.float32)


NN, NT, TN = ((1,), (0,)), ((1,), (1,)), ((0,), (0,))


def layer_kernel(
    sizes, rows_per, layer_in, norm_attn, norm_moe, table_t, router_t, info_ref, cot_ref,
    wq_hbm, wk_hbm, wv_hbm, wo_hbm, wg_hbm, wu_hbm, wd_hbm,
    q_out, x_ref, hid_out, dg_out, du_out, gr_out, query, key, value, probs, context, residual, attn_in, gate_out,
    g_ref, w_ref, weights, act, slope, away, own, sem_a, sem_w, *scratch,
):
    me = Place(*sizes)
    c = me.c
    seq, width = layer_in.shape
    heads, buckets = table_t.shape
    units = wg_hbm.shape[1]
    bf, f32 = jnp.bfloat16, jnp.float32

    attn_w = []
    for i, src in enumerate((wq_hbm, wk_hbm, wv_hbm, wo_hbm)):
        dst = weights.at[pl.ds(i * width, width)]
        attn_w.append(pltpu.make_async_copy(src, dst, sem_a.at[i]))
        attn_w[-1].start()
    greet(column_peers(me))
    rows_in = rows_of(me, rows_per, scratch[:8])
    info_all, gates, tok = scratch[:3]
    buf_x, buf_w, buf_g = scratch[5:8]
    out_x, out_w, out_g = [
        Spread(me, buf, recv, [s.at[i] for s in scratch[8:14]])
        for i, (buf, recv) in enumerate(((buf_x, x_ref), (buf_w, w_ref), (buf_g, g_ref)))
    ]
    scratch = scratch[14:]
    column = me.n_expert
    quarter = [range(i * column // 4, (i + 1) * column // 4) for i in range(4)]
    info_all[c] = info_ref[...]
    rows_in.share("info", info_all)
    tok[1, c] = cot_ref[...]
    rows_in.share(1, tok.at[1])
    rows = layer_in[...].astype(f32)
    attn_in[...] = (rows * row_scale(rows) * norm_attn[...]).astype(bf)
    rows_in.hots()
    buf_g[...] = rows_in.gather(1)
    out_g.send()
    for i, ref in enumerate((query, key, value)):
        attn_w[i].wait()
        ref[...] = dot_as(attn_in[...], weights[i * width : (i + 1) * width, :], NN).astype(bf)
    relative = lax.broadcasted_iota(jnp.int32, (heads, 2 * seq), 1) - seq
    bucket = bucket_of(relative)
    bias_of = jnp.zeros((heads, 2 * seq), f32)
    for n in range(buckets):
        bias_of = jnp.where(bucket == n, table_t[:, n : n + 1], bias_of)
    pair = 2 * width // heads
    low_half = lax.broadcasted_iota(jnp.int32, (seq, pair), 1) < pair // 2
    for n in range(heads // 2):
        lanes = slice(n * pair, (n + 1) * pair)
        k2, v2 = key[:, lanes], value[:, lanes]
        total = None
        for h in range(2):
            mine = low_half if h == 0 else ~low_half
            head = 2 * n + h
            line = jnp.broadcast_to(bias_of[head : head + 1, :], (seq, 2 * seq))
            bias = pltpu.roll(line, seq, 1, stride=1, stride_axis=0)[:, :seq]
            scores = dot_as(query[:, lanes], jnp.where(mine, k2, jnp.zeros_like(k2)), NT) + bias
            exponent = jnp.exp(scores - jnp.max(scores, axis=-1, keepdims=True))
            prob = exponent / jnp.sum(exponent, axis=-1, keepdims=True)
            probs[head] = prob
            term = dot_as(prob.astype(bf), jnp.where(mine, v2, jnp.zeros_like(v2)), NN)
            total = term if total is None else total + term
        context[:, lanes] = total.astype(bf)
        if n % 4 == 3:
            out_g.pass_on(quarter[n // 4])
    attn_w[3].wait()
    resid = rows + dot_as(context[...], weights[3 * width : 4 * width, :], NN)
    residual[...] = resid
    fetch = {}
    for n, j in enumerate((c, 1 - c)):
        for i, src in enumerate((wg_hbm, wu_hbm, wd_hbm)):
            dst = weights.at[pl.ds(pl.multiple_of((2 * i + j) * units, 16), units)]
            fetch[n, i] = pltpu.make_async_copy(src.at[j], dst, sem_w.at[n, i])
            fetch[n, i].start()
    moe_in = resid * row_scale(resid) * norm_moe[...]
    tok[0, c] = moe_in.astype(bf)
    rows_in.share(0, tok.at[0])
    logits = lax.dot_general(
        router_t[...], moe_in, (NT, ((), ())), preferred_element_type=f32, precision=highest
    )
    logits = jnp.exp(logits - jnp.max(logits, axis=0, keepdims=True))
    gate_prob = logits / jnp.sum(logits, axis=0, keepdims=True)
    expert_ids = lax.broadcasted_iota(jnp.int32, gate_prob.shape, 0)
    picked = [
        jnp.sum(jnp.where(info_ref[k : k + 1, :] == expert_ids, gate_prob, 0.0), axis=0, keepdims=True)
        for k in range(2)
    ]
    both = picked[0] + picked[1]
    for k in range(2):
        gates[c, k : k + 1, :] = picked[k] / both
    gates[c, 2:, :] = jnp.zeros((6, seq), f32)
    gate_out[...] = gates[c]
    rows_in.share("gates", gates)
    buf_x[...] = rows_in.gather(0)
    out_x.send()
    out_g.pass_on(quarter[2])
    for e, tile in enumerate(rows_in.weights()):
        buf_w[e] = tile
    out_w.send()
    out_g.pass_on(quarter[3])
    out_g.cross(0)

    size = x_ref.shape[2]
    step = math.gcd(column, 4)
    chunk = step * size
    back = Back(
        me, lambda i: away.at[i],
        lambda i, block: own[i, pl.ds(pl.multiple_of(block * size, 8), size), :],
        q_out, *scratch[:4], scratch[4:],
    )

    def part(i, j):
        return weights[pl.ds(pl.multiple_of((2 * i + j) * units, 16), units), :]

    def flat(value):
        return value.reshape(chunk, value.shape[-1])

    def blocks(value):
        return value.reshape(step, size, value.shape[-1])

    def store(i, first, some, rows, value):
        if first:
            away[i, some] = blocks(value.astype(bf))
        else:
            own[i, rows, :] = value

    def each(start, count, body):
        @pl.loop(0, count // step)
        def _(n):
            at = start + n * step
            body(pl.ds(at, step), pl.ds(pl.multiple_of(at * size, 8), chunk))

    def forward(first, j, start, count):
        def body(some, rows):
            x = flat(x_ref[j, some])
            gate_pre = dot_as(x, part(0, j), NT)
            up_pre = dot_as(x, part(1, j), NT)
            hidden, active, lean = gated_terms(gate_pre, up_pre)
            act[j, rows, :] = active
            slope[j, rows, :] = lean
            hidden = hidden.astype(bf)
            hid_out[j, some] = blocks(hidden)
            store(0, first, some, rows, dot_as(hidden, part(2, j), NN))

        each(start, count, body)

    lane = lax.broadcasted_iota(jnp.int32, (size, 128), 1)
    row = lax.broadcasted_iota(jnp.int32, (size, 128), 0)

    def backward(first, j, start, count):
        def body(some, rows):
            tiles = w_ref[j, some]
            grad = []
            for n in range(step):
                line = jnp.broadcast_to(tiles[n, 0:1, :], (size, 128))
                weight = jnp.sum(jnp.where(lane == row, line, 0.0), axis=1, keepdims=True)
                grad.append(weight * g_ref[j, some.start + n].astype(f32))
            grad = jnp.concatenate(grad, axis=0).astype(bf)
            gr_out[j, some] = blocks(grad)
            grad_hidden = dot_as(grad, part(2, j), NT)
            dg = (grad_hidden * slope[j, rows, :]).astype(bf)
            du = (grad_hidden * act[j, rows, :]).astype(bf)
            dg_out[j, some] = blocks(dg)
            du_out[j, some] = blocks(du)
            store(1, first, some, rows, dot_as(dg, part(0, j), NN) + dot_as(du, part(1, j), NN))

        each(start, count, body)

    here = me.y * column
    away_ys = [back.ys[k] * column for k in range(1, me.ny)]
    shares = [back.order[i * column // 4 : (i + 1) * column // 4] for i in range(4)]
    out_x.pass_on(range(column))
    out_x.cross(0)
    for s in range(1, me.ny):
        out_g.cross(s)
    for i in range(3):
        fetch[0, i].wait()
    forward(False, c, here, column)
    for i in range(3):
        fetch[1, i].wait()
    out_x.crossed[0].wait_recv()
    forward(True, 1 - c, here, column)
    back.to_mate(0, 0)
    out_w.pass_column()
    out_w.cross(0)
    for s in range(1, me.ny):
        out_x.cross(s)
    for k in range(1, me.ny):
        out_x.crossed[k].wait_recv()
        forward(True, 1 - c, away_ys[k - 1], column)
        back.to_mate(0, k)
    for s in range(1, me.ny):
        out_w.cross(s)
    for k in range(1, me.ny):
        forward(False, c, away_ys[k - 1], column)
    back.along_y(0)
    out_g.arrive()
    out_w.arrive()
    for k in range(1, me.ny):
        backward(True, 1 - c, away_ys[k - 1], column)
        back.to_mate(1, k)
    back.finish(0, shares[0])
    for k in range(1, me.ny):
        backward(False, c, away_ys[k - 1], column)
    back.along_y(1)
    back.finish(0, shares[1])
    backward(True, 1 - c, here, column)
    back.to_mate(1, 0)
    back.finish(0, shares[2])
    backward(False, c, here, column)
    back.finish(0, shares[3])
    back.across(0)
    back.finish(1, back.order)
    back.across(1)
    back.close()
    for payload in (out_x, out_w, out_g):
        payload.close()
    rows_in.close()


def layer(sizes, micro, cap, layer_in, norms, table_t, router_t, info, cot, attn_w, expert_w):
    n_expert, ny, per_core = sizes[0], sizes[1] // 2, micro * cap
    seq, width = cot.shape
    units = expert_w[0].shape[1]
    heads = table_t.shape[0]
    count, size = ny * n_expert, 2 * per_core
    bf, f32 = jnp.bfloat16, jnp.float32
    any_space = pl.BlockSpec(memory_space=pl.ANY)
    inner = jax.ShapeDtypeStruct((2, count, size, units), bf)
    outer = jax.ShapeDtypeStruct((2, count, size, width), bf)
    low, full = jax.ShapeDtypeStruct((seq, width), bf), jax.ShapeDtypeStruct((seq, width), f32)
    return pl.pallas_call(
        functools.partial(layer_kernel, sizes, (micro, cap, per_core)),
        out_shape=(
            jax.ShapeDtypeStruct((2, 2, n_expert, size, width), bf), outer, inner, inner, inner, outer,
            low, low, low, jax.ShapeDtypeStruct((heads, seq, seq), f32), low, full, low,
            jax.ShapeDtypeStruct((8, seq), f32),
        ),
        in_specs=[VMEM] * 7 + [any_space] * 7,
        out_specs=(VMEM,) * 14,
        scratch_shapes=[
            pltpu.VMEM((2, count, size, width), bf),
            pltpu.VMEM((2, count, 8, 128), f32),
            pltpu.VMEM((max(4 * width, 6 * units), width), bf),
            pltpu.VMEM((2, count * size, units), f32),
            pltpu.VMEM((2, count * size, units), f32),
            pltpu.VMEM((2, count, size, width), bf),
            pltpu.VMEM((2, count * size, width), f32),
            DMA((4,)),
            DMA((2, 3)),
        ]
        + rows_scratch(sizes, per_core, seq, width)
        + spread_sems(sizes)
        + back_scratch(sizes, size, width),
        name="layer",
        compiler_params=pltpu.CompilerParams(
            collective_id=4, has_side_effects=True, vmem_limit_bytes=54 << 20
        ),
    )(layer_in, *norms, table_t, router_t, info, cot, *attn_w, *expert_w)


def finish_kernel(sums_hbm, x_hbm, h_hbm, dg_hbm, du_hbm, gr_hbm, *refs):
    outs, (sums, x, h, dg, du, gr, stage, sem_sum, sem_in, sem_out) = refs[:7], refs[7:]
    slots, rows = stage.shape[:2]
    width = sums.shape[1]
    units = h.shape[2]
    loads = {}

    def load(key, src, dst, sem):
        loads[key] = pltpu.make_async_copy(src, dst, sem)
        loads[key].start()

    def load_sums(keys):
        for n in keys:
            part = n * rows // width, pl.ds(n * rows % width, rows)
            load(("sums", n), sums_hbm.at[part], sums.at[part], sem_sum.at[n])

    casts = range(4 * width // rows)
    load_sums(casts[:4])
    for i, (key, src, dst) in enumerate(
        (("dg", dg_hbm, dg), ("x", x_hbm, x), ("du", du_hbm, du), ("h", h_hbm, h), ("gr", gr_hbm, gr))
    ):
        for j in range(2):
            load((key, j), src.at[j], dst.at[j], sem_in.at[i, j])
    load_sums(casts[4:])

    def need(key):
        if key in loads:
            loads.pop(key).wait()

    jobs = []
    products = [
        (left, right, out, j, f)
        for left, right, out in ((("dg", dg), ("x", x), 4), (("du", du), ("x", x), 5), (("h", h), ("gr", gr), 6))
        for j in range(2)
        for f in range(0, units, rows)
    ]
    casts = list(casts)
    while casts or products:
        if casts:
            jobs.append(casts.pop(0))
        if products and (len(jobs) > 3 or not casts):
            jobs.append(products.pop(0))
    flying = [None] * slots
    for n, job in enumerate(jobs):
        slot = n % slots
        if flying[slot] is not None:
            flying[slot].wait()
        if isinstance(job, int):
            need(("sums", job))
            m, r = job * rows // width, job * rows % width
            stage[slot] = sums[m, r : r + rows, :].astype(jnp.float32)
            src, dst = stage.at[slot], outs[m].at[pl.ds(r, rows)]
        else:
            (left_key, left), (right_key, right), out, j, f = job
            need((left_key, j))
            need((right_key, j))
            size = min(rows, units - f)
            stage[slot, :size] = lax.dot_general(
                left[j, :, f : f + size], right[j], (((0,), (0,)), ((), ())),
                preferred_element_type=jnp.float32,
            )
            src, dst = stage.at[slot, pl.ds(0, size)], outs[out].at[j, pl.ds(f, size)]
        flying[slot] = pltpu.make_async_copy(src, dst, sem_out.at[slot])
        flying[slot].start()
    for copy in flying:
        if copy is not None:
            copy.wait()


def finish(sums, x, h, dg, du, gr):
    f32 = jnp.float32
    width = sums.shape[1]
    units = h.shape[2]
    any_space = pl.BlockSpec(memory_space=pl.ANY)
    return pl.pallas_call(
        finish_kernel,
        out_shape=(jax.ShapeDtypeStruct((width, width), f32),) * 4
        + (jax.ShapeDtypeStruct((2, units, width), f32),) * 3,
        in_specs=[any_space] * 6,
        out_specs=(any_space,) * 7,
        scratch_shapes=[pltpu.VMEM(a.shape, a.dtype) for a in (sums, x, h, dg, du, gr)]
        + [pltpu.VMEM((6, 256, width), f32), DMA((4 * width // 256,)), DMA((5, 2)), DMA((6,))],
        name="finish",
        compiler_params=pltpu.CompilerParams(vmem_limit_bytes=60 << 20),
    )(sums, x, h, dg, du, gr)


def reduce_kernel(
    sizes, pieces, left_ref, right_ref, small_ref, out_hbm, small_out,
    out, sem_out, buf_a, buf_b, acc, *boxes,
):
    me = Place(*sizes)
    c, mate = me.c, me.at(c=1 - me.c)
    n = me.nx
    seq = right_ref.shape[1]
    total_rows = out.shape[1]
    is0 = c == 0
    pair = jnp.where(is0, me.x, me.y)
    other = jnp.where(is0, me.y, me.x)
    lo, hi, nh = pair % 2, pair // 2, n // 2

    def along(pair_at, other_at, z=None):
        return me.at(x=jnp.where(is0, pair_at, other_at), y=jnp.where(is0, other_at, pair_at), z=z)

    flip_x, flip_y = me.x + 1 - 2 * (me.x % 2), me.y + 1 - 2 * (me.y % 2)
    dims = [
        (n, other, lambda q: along(pair, q)),
        (nh, hi, lambda q: along(q * 2 + lo, other)),
        (2, me.z % 2, lambda q: me.at(z=me.z // 2 * 2 + q)),
        (me.nz // 2, me.z // 2, lambda q: me.at(z=q * 2 + me.z % 2)),
    ]
    parts, gots = boxes[:4], boxes[4:8]
    half, small_half, small_got, fs, fr, os, ps, pr, gs, gr, ms, mr, cs, cr, ss, sr = boxes[8:]
    levels = [i for i, d in enumerate(dims) if d[0] > 1]
    x_peers = [me.at(x=(me.x + k) % n) for k in range(1, n)]
    y_peers = [me.at(y=(me.y + k) % n) for k in range(1, n)]
    z_peers = [me.at(z=(me.z + k) % me.nz) for k in range(1, me.nz)]
    greet(
        [mate, me.at(x=flip_x, c=1 - c), me.at(y=flip_y, c=1 - c)] + x_peers + y_peers + z_peers
    )

    def slot_a(slot):
        return buf_a.at[pl.ds(pl.multiple_of(slot * seq, seq), seq), :]

    def slot_b(slot):
        return buf_b.at[pl.ds(pl.multiple_of(slot * seq, seq), seq), :]

    targets = [
        (mate, 1 - c, other % 2, c),
        (me.at(x=flip_x, c=0), 0, flip_x % 2, 2 + c),
        (me.at(y=flip_y, c=1), 1, flip_y % 2, 2 + c),
    ]
    factor = []
    for i, (device, role, parity, slot) in enumerate(targets):
        a, b = jnp.where(role == 0, 0, parity), role * 2 + parity
        factor.append(remote(left_ref.at[a], slot_a(slot), fs.at[i, 0], fr.at[slot, 0], device))
        factor.append(remote(right_ref.at[b], slot_b(slot), fs.at[i, 1], fr.at[slot, 1], device))
    own = [
        pltpu.make_async_copy(left_ref.at[jnp.where(is0, 0, lo)], slot_a(c), os.at[0]),
        pltpu.make_async_copy(right_ref.at[c * 2 + lo], slot_b(c), os.at[1]),
    ]
    for copy in own:
        copy.start()
    rows_s = half.shape[0]
    small = [remote(small_ref.at[pl.ds((1 - c) * rows_s, rows_s)], half, ss.at[0], sr.at[0], mate)]
    small_dims = [
        (n, me.x, lambda q: me.at(x=q)),
        (n, me.y, lambda q: me.at(y=q)),
        (me.nz, me.z, lambda q: me.at(z=q)),
    ]
    small_wait = [small[0]]
    small_slot = [1]

    def small_step(step):
        for copy in small_wait:
            copy.wait_recv()
        small_wait.clear()
        if step == 0:
            total = small_ref[pl.ds(c * rows_s, rows_s)] + half[...]
        elif step <= 3:
            total = small_got[step - 1, 0]
            for k in range(1, small_dims[step - 1][0]):
                total = total + small_got[step - 1, k]
        if step < 3:
            count, index, peer = small_dims[step]
            small_half[step] = total
            small_got[step, index] = total
            for k in range(1, count):
                small_wait.append(
                    remote(
                        small_half.at[step], small_got.at[step, index], ss.at[small_slot[0]],
                        sr.at[small_slot[0]], peer((index + k) % count),
                    )
                )
                small_slot[0] += 1
        elif step == 3:
            small_out[pl.ds(c * rows_s, rows_s)] = total
            block = small_out.at[pl.ds(c * rows_s, rows_s)]
            small_wait.append(
                remote(block, block, ss.at[small_slot[0]], sr.at[small_slot[0]], mate)
            )
        small.extend(small_wait)

    for where in (1 - c, 2, 3):
        for i, (src, dst) in enumerate(((left_ref, slot_a(where)), (right_ref, slot_b(where)))):
            pltpu.make_async_remote_copy(
                src_ref=src.at[0], dst_ref=dst, send_sem=fs.at[0, i], recv_sem=fr.at[where, i],
                device_id=mate, device_id_type=MESH,
            ).wait_recv()
    for copy in own:
        copy.wait()

    rows_k = total_rows // pieces
    matrix = c * 2 + lo
    pending, written = {}, []

    def multiply(k):
        acc[k] = lax.dot_general(
            buf_a[:, k * rows_k : (k + 1) * rows_k], buf_b[...], (((0,), (0,)), ((), ())),
            preferred_element_type=jnp.float32,
        )
        push(k, 0, rows_k)

    def push(k, at, rows):
        level = levels[at]
        count, index, peer = dims[level]
        size = rows // count
        copies = []
        for s in range(1, count):
            to = (index + s) % count
            parts[level][k, s - 1] = acc[k, pl.ds(pl.multiple_of(to * size, 8), size), :].astype(jnp.bfloat16)
            copies.append(
                remote(
                    parts[level].at[k, s - 1], gots[level].at[k, s - 1],
                    ps.at[level, k, s - 1], pr.at[level, k, s - 1], peer(to),
                )
            )
        pending["push", at, k] = copies

    def rows_at(at):
        rows = rows_k
        for i in range(at):
            rows //= dims[levels[i]][0]
        return rows

    def add(k, at):
        level = levels[at]
        count, index, _ = dims[level]
        size = rows_at(at) // count
        for copy in pending["push", at, k]:
            copy.wait_recv()
        total = acc[k, pl.ds(pl.multiple_of(index * size, 8), size), :]
        for s in range(1, count):
            total = total + gots[level][k, s - 1].astype(jnp.float32)
        if at + 1 < len(levels):
            acc[k, :size, :] = total
            push(k, at + 1, size)
        else:
            out[matrix, pl.ds(offset(k, at), size), :] = total.astype(jnp.bfloat16)
            share(k, at)

    def offset(k, at):
        start, rows = k * rows_k, rows_k
        for i in range(at + 1):
            count, index, _ = dims[levels[i]]
            rows //= count
            start = start + index * rows
        return pl.multiple_of(start, 8)

    def share(k, at):
        level = levels[at]
        count, index, peer = dims[level]
        size = rows_at(at) // count
        block = out.at[matrix, pl.ds(offset(k, at), size), :]
        pending["share", at, k] = [
            remote(block, block, gs.at[level, k, s - 1], gr.at[level, k, s - 1], peer((index + s) % count))
            for s in range(1, count)
        ]

    def shared(k, at):
        for copy in pending["share", at, k]:
            copy.wait_recv()
        if at:
            share(k, at - 1)
        else:
            block = out.at[matrix, pl.ds(k * rows_k, rows_k), :]
            pending["mate", k] = remote(
                block, block, ms.at[k], mr.at[k], along(pair + 1 - 2 * lo, other)
            )

    def across(k):
        pending["mate", k].wait_recv()
        block = out.at[pl.ds(2 * c, 2), pl.ds(k * rows_k, rows_k), :]
        pending["core", k] = remote(block, block, cs.at[k], cr.at[k], mate)
        write(k, c)

    def write(k, core):
        part = pl.ds(2 * core, 2), pl.ds(k * rows_k, rows_k), slice(None)
        written.append(pltpu.make_async_copy(out.at[part], out_hbm.at[part], sem_out.at[core, k]))
        written[-1].start()

    def close(k):
        pending["core", k].wait_recv()
        write(k, 1 - c)

    steps = [multiply]
    steps += [functools.partial(add, at=i) for i in range(len(levels))]
    steps += [functools.partial(shared, at=i) for i in reversed(range(len(levels)))]
    events = sorted((0 if p == 0 else p + k, p, k) for p in range(len(steps)) for k in range(pieces))
    before = 0
    for t, p, k in events:
        if before < t <= 5:
            small_step(t - 1)
        before = t
        steps[p](k)
    for k in range(pieces):
        across(k)
    for k in range(pieces):
        close(k)
    for copy in factor + small:
        copy.wait_send()
    for copies in pending.values():
        for copy in copies if isinstance(copies, list) else [copies]:
            copy.wait_send()
    for copy in written:
        copy.wait()


def reduce_all(sizes, left, right, small, pieces=8):
    n_expert, n_dp = sizes
    nz = math.gcd(n_expert, 4)
    n = n_expert // nz
    nh = n // 2
    assert n == n_dp // 2
    seq, width = left.shape[1:]
    rows_k = width // pieces
    bf, f32 = jnp.bfloat16, jnp.float32
    rows_s = small.shape[0] // 2
    splits = [n, nh, 2, nz // 2]
    sizes_at = [rows_k // math.prod(splits[: i + 1]) for i in range(4)]
    counts = [max(q - 1, 1) for q in splits]
    most = max(counts)
    boxes = [pltpu.VMEM((pieces, q, s, width), bf) for q, s in zip(counts, sizes_at)]
    smalls = 2 * n + nz
    return pl.pallas_call(
        functools.partial(reduce_kernel, sizes, pieces),
        out_shape=(
            jax.ShapeDtypeStruct((4, width, width), bf),
            jax.ShapeDtypeStruct(small.shape, f32),
        ),
        in_specs=[VMEM] * 3,
        out_specs=(pl.BlockSpec(memory_space=pl.ANY), VMEM),
        scratch_shapes=[
            pltpu.VMEM((4, width, width), bf),
            DMA((2, pieces)),
            pltpu.VMEM((4 * seq, width), bf),
            pltpu.VMEM((4 * seq, width), bf),
            pltpu.VMEM((pieces, rows_k, width), f32),
            *boxes,
            *boxes,
            pltpu.VMEM((rows_s, width), f32),
            pltpu.VMEM((3, rows_s, width), f32),
            pltpu.VMEM((3, max(n, nz), rows_s, width), f32),
            DMA((3, 2)),
            DMA((4, 2)),
            DMA((2,)),
            DMA((4, pieces, most)),
            DMA((4, pieces, most)),
            DMA((4, pieces, most)),
            DMA((4, pieces, most)),
            DMA((pieces,)),
            DMA((pieces,)),
            DMA((pieces,)),
            DMA((pieces,)),
            DMA((smalls,)),
            DMA((smalls,)),
        ],
        name="reduce_all",
        compiler_params=pltpu.CompilerParams(
            collective_id=3, has_side_effects=True, vmem_limit_bytes=56 << 20
        ),
    )(left, right, small)


def rms_scale(values):
    return lax.rsqrt(jnp.mean(values * values, axis=-1, keepdims=True) + epsilon)


def bucket_hot(seq_len, buckets):
    position = jnp.arange(seq_len, dtype=jnp.int32)
    relative = position[None, :] - position[:, None]
    distance = jnp.abs(relative)
    far_bucket = jnp.full_like(distance, 8)
    for threshold in bucket_edges:
        far_bucket = far_bucket + (distance >= threshold).astype(jnp.int32)
    bucketed = jnp.where(distance < 8, distance, far_bucket) + 16 * (relative > 0).astype(jnp.int32)
    bucket_ids = jnp.arange(buckets, dtype=jnp.int32)
    return (bucketed[None, :, :] == bucket_ids[:, None, None]).astype(jnp.float32)


def dot32(pattern, left, right):
    return jnp.einsum(pattern, left, right, preferred_element_type=jnp.float32)


def shards(
    layer_in, routes, queue_slots, norm_attn, w_query, w_key, w_value, w_out, rel_table,
    norm_moe, router, w_gate, w_up, w_down, cotangent,
):
    bf, f32 = jnp.bfloat16, jnp.float32
    seq_len, width = layer_in.shape
    buckets, heads = rel_table.shape
    expert_count = router.shape[1]
    sizes = (lax.axis_size("expert"), lax.axis_size("dp"))
    n_expert, n_dp = sizes
    assert w_gate.shape[0] == 2 and expert_count == 2 * n_expert
    group_len = seq_len // MICRO
    capacity = (5 * group_len + 2 * expert_count - 1) // (2 * expert_count)
    split_heads = (seq_len, heads, width // heads)
    layer_rows = layer_in.astype(f32)
    inv_attn = rms_scale(layer_rows)
    normed_attn = layer_rows * inv_attn
    one_hot = bucket_hot(seq_len, buckets)
    info = jnp.concatenate([routes.T, queue_slots.T, jnp.zeros((4, seq_len), jnp.int32)])
    expert_w = [jnp.swapaxes(w_gate, 1, 2), jnp.swapaxes(w_up, 1, 2), w_down]
    slots = n_dp // 2 * n_expert * 2 * MICRO * capacity
    fused = 2 * slots * width * 20 + 6 * w_gate.size < 52 << 20
    if fused:
        (
            back, rows_in, hidden, gate_grad, up_grad, grad_rows,
            query, key, value, probs, context, residual, attn_in, gates,
        ) = layer(
            sizes, MICRO, capacity, layer_in, (norm_attn[None], norm_moe[None]), rel_table.T, router.T,
            info, cotangent, (w_query, w_key, w_value, w_out), expert_w,
        )
    else:
        attn_in = (normed_attn * norm_attn).astype(bf)
        query = dot32("sd,de->se", attn_in, w_query).astype(bf)
        key = dot32("sd,de->se", attn_in, w_key).astype(bf)
        value = dot32("sd,de->se", attn_in, w_value).astype(bf)
        bias = jnp.einsum("bij,bh->hij", one_hot, rel_table, precision=highest)
        scores = dot32("ihd,jhd->hij", query.reshape(split_heads), key.reshape(split_heads)) + bias
        exponent = jnp.exp(scores - jnp.max(scores, axis=-1, keepdims=True))
        probs = exponent / jnp.sum(exponent, axis=-1, keepdims=True)
        context = dot32("hij,jhd->ihd", probs.astype(bf), value.reshape(split_heads))
        context = context.astype(bf).reshape(seq_len, width)
        residual = layer_rows + dot32("se,ed->sd", context, w_out)
    inv_moe = rms_scale(residual)
    normed_moe = residual * inv_moe
    moe_in = normed_moe * norm_moe
    expert_ids = jnp.arange(expert_count, dtype=jnp.int32)
    first_hot = (routes[:, 0:1] == expert_ids).astype(f32)
    second_hot = (routes[:, 1:2] == expert_ids).astype(f32)
    if not fused:
        gate_prob = jax.nn.softmax(jnp.dot(moe_in, router, precision=highest), axis=-1)
        prob_first, prob_second = jnp.sum(gate_prob * first_hot, axis=-1), jnp.sum(gate_prob * second_hot, axis=-1)
        gates = jnp.stack([prob_first, prob_second]) / (prob_first + prob_second)
        gates = jnp.pad(gates, ((0, 6), (0, 0)))
        rows_in, weight_in, grad_in = spread(
            sizes, MICRO, capacity, info, moe_in.astype(bf), cotangent, gates
        )
        blocks = rows_in.shape[:-1] + (-1,)
        rows_in, grad_in = [a.reshape(2, -1, width) for a in (rows_in, grad_in)]
        slot_weight = weight_in[:, :, 0, : 2 * MICRO * capacity].reshape(2, -1, 1)
        grad_rows = (slot_weight * grad_in.astype(f32)).astype(bf)
        gate_pre = dot32("jrd,jdf->jrf", rows_in, w_gate)
        up_pre = dot32("jrd,jdf->jrf", rows_in, w_up)
        hidden, active, lean = gated_terms(gate_pre, up_pre)
        hidden = hidden.astype(bf)
        partial_out = dot32("jrf,jfd->jrd", hidden, w_down).astype(bf)
        hidden_grad = dot32("jrd,jfd->jrf", grad_rows, w_down)
        gate_grad, up_grad = (hidden_grad * lean).astype(bf), (hidden_grad * active).astype(bf)
        rows_grad = dot32("jrf,jdf->jrd", gate_grad, w_gate) + dot32("jrf,jdf->jrd", up_grad, w_up)
        back = gather_back(sizes, partial_out.reshape(blocks), rows_grad.astype(bf).reshape(blocks))
    weight_first, weight_second = gates[0][:, None], gates[1][:, None]
    query_heads, key_heads, value_heads = [a.reshape(split_heads) for a in (query, key, value)]
    probs_low = probs.astype(bf)
    rows_in, hidden, gate_grad, up_grad, grad_rows = [
        a.reshape(2, -1, a.shape[-1]) for a in (rows_in, hidden, gate_grad, up_grad, grad_rows)
    ]
    back = back.reshape(2, -1, width)

    core = lax.axis_index("dp") % 2
    per_core = MICRO * capacity
    token = jnp.arange(seq_len, dtype=jnp.int32)[:, None]
    place = (routes % 2) * (n_expert * 2 * per_core) + (routes // 2) * (2 * per_core)
    place = place + core * per_core + (token // group_len) * capacity + queue_slots
    place = jnp.where(queue_slots >= 0, place, -1)
    slot_ids = jnp.arange(2 * n_expert * 2 * per_core, dtype=jnp.int32)
    select_first = (place[:, 0:1] == slot_ids).astype(bf)
    select_second = (place[:, 1:2] == slot_ids).astype(bf)
    picked_first = dot32("tp,pd->td", select_first, back[0])
    picked_second = dot32("tp,pd->td", select_second, back[0])
    moe = weight_first * picked_first + weight_second * picked_second
    layer_out = (residual + moe).astype(bf)
    cot_rows = cotangent.astype(f32)
    grad_weight_first = jnp.sum(cot_rows * picked_first, axis=-1, keepdims=True)
    grad_weight_second = jnp.sum(cot_rows * picked_second, axis=-1, keepdims=True)
    grad_from_slots = dot32("tp,pd->td", select_first + select_second, back[1])
    mean_grad = weight_first * grad_weight_first + weight_second * grad_weight_second
    logit_first = weight_first * (grad_weight_first - mean_grad)
    logit_second = weight_second * (grad_weight_second - mean_grad)
    grad_logits = logit_first * first_hot + logit_second * second_hot
    grad_router = jnp.einsum("sd,se->ed", moe_in, grad_logits, precision=highest)
    grad_moe_in = grad_from_slots + jnp.einsum("se,de->sd", grad_logits, router, precision=highest)
    grad_norm_moe = jnp.sum(grad_moe_in * normed_moe, axis=0)
    grad_normed = grad_moe_in * norm_moe
    grad_residual = cot_rows + inv_moe * (
        grad_normed - normed_moe * jnp.mean(grad_normed * normed_moe, axis=-1, keepdims=True)
    )
    grad_attn_low = grad_residual.astype(bf)
    grad_context = dot32("sd,ed->se", grad_attn_low, w_out).astype(bf).reshape(split_heads)
    grad_values = dot32("hij,ihd->jhd", probs_low, grad_context).astype(bf).reshape(seq_len, width)
    grad_probs = dot32("ihd,jhd->hij", grad_context, value_heads)
    grad_scores = probs * (grad_probs - jnp.sum(probs * grad_probs, axis=-1, keepdims=True))
    grad_rel_table = jnp.einsum("bij,hij->bh", one_hot, grad_scores, precision=highest)
    scores_low = grad_scores.astype(bf)
    grad_queries = dot32("hij,jhd->ihd", scores_low, key_heads).astype(bf).reshape(seq_len, width)
    grad_keys = dot32("hij,ihd->jhd", scores_low, query_heads).astype(bf).reshape(seq_len, width)
    grad_attn_in = dot32("se,de->sd", grad_queries, w_query)
    grad_attn_in = grad_attn_in + dot32("se,de->sd", grad_keys, w_key)
    grad_attn_in = grad_attn_in + dot32("se,de->sd", grad_values, w_value)
    grad_norm_attn = jnp.sum(grad_attn_in * normed_attn, axis=0)
    grad_normed_attn = grad_attn_in * norm_attn
    grad_input = grad_residual + inv_attn * (
        grad_normed_attn
        - normed_attn * jnp.mean(grad_normed_attn * normed_attn, axis=-1, keepdims=True)
    )
    table = grad_rel_table.reshape(-1)
    small = jnp.concatenate(
        [
            grad_router,
            grad_norm_attn[None],
            grad_norm_moe[None],
            jnp.pad(table, (0, width - table.size))[None],
        ]
    )
    small = jnp.pad(small, ((0, -small.shape[0] % 16), (0, 0)))
    sums, small = reduce_all(
        sizes,
        jnp.stack([attn_in, context]),
        jnp.stack([grad_queries, grad_keys, grad_values, grad_attn_low]),
        small,
    )
    *matrices, grad_w_gate, grad_w_up, grad_w_down = finish(
        sums, rows_in, hidden, gate_grad, up_grad, grad_rows
    )
    grad_w_gate, grad_w_up = jnp.swapaxes(grad_w_gate, 1, 2), jnp.swapaxes(grad_w_up, 1, 2)
    return (
        layer_out, grad_input, small[expert_count], *matrices,
        small[expert_count + 2, : table.size].reshape(buckets, heads),
        small[expert_count + 1], small[:expert_count].T, grad_w_gate, grad_w_up, grad_w_down,
    )


def solution(mesh):
    in_specs = (
        P(("expert", "dp"), None),
        P(("expert", "dp"), None),
        P(("expert", "dp"), None),
        P(),
        P(),
        P(),
        P(),
        P(),
        P(),
        P(),
        P(),
        P("expert", None, "dp"),
        P("expert", None, "dp"),
        P("expert", "dp", None),
        P(("expert", "dp"), None),
    )
    out_specs = (
        P(("expert", "dp"), None),
        P(("expert", "dp"), None),
        P(),
        P(),
        P(),
        P(),
        P(),
        P(),
        P(),
        P(),
        P("expert", None, "dp"),
        P("expert", None, "dp"),
        P("expert", "dp", None),
    )
    return jax.shard_map(shards, mesh=mesh, in_specs=in_specs, out_specs=out_specs, check_vma=False)
```

profile of v0, /device:TPU:1, one launch (start us, length us, event | category | flops | bytes accessed | tf_op | source)
XLA Modules:
  0.0 251.3 jit_solution(2576793599437530174)
XLA Ops:
  0.7 1.1 fusion.12
  2.3 0.7 compare_select_fusion.1
  3.1 0.8 slice_bitcast_fusion.2
  3.8 1.4 add_add_fusion.info_ref
  5.3 99.8 %layer.1 = (bf16[2,2,8,40,1024]{4,3,2,1,0:T(8,128)(2,1)}, bf16[2,16,40,1024]{3,2,1,0:T(8,128)(2,1)}, bf16[2,16,40,704]{3,2,1,0:T(8,128)(2,1)}, bf16[2,16,40,704]...) custom-call(bf16[128,1024]{1,0:T(8,128)(2,1)} %layer_in.1, ...), custom_call_target="tpu_custom_call" | custom-call | tf_op jit(solution)/shard_map/layer/pallas_call | solution.py:660
  105.0 2.0 fusion.61
  107.1 1.9 copy.40
  109.0 1.8 copy.42
  110.8 1.8 copy.45
  113.0 1.2 fusion.13
  114.7 0.6 fusion.45
  115.4 0.6 multiply_reduce_fusion.1
  116.0 0.9 convert_bitcast_fusion
  117.0 0.8 convolution_convert_fusion.3
  118.4 0.9 copy.48
  119.3 0.8 pad_maximum_fusion.1.left_ref
  121.0 1.6 fusion.1
  123.5 0.9 copy.47
  124.3 0.8 copy.46
  125.2 2.4 pad_maximum_fusion.right_ref
  127.6 0.8 fusion.63
  128.5 0.8 convolution_add_fusion.2
  129.3 0.7 copy-done.4
  130.0 1.0 fusion.11
  131.0 1.0 fusion.10
  132.1 0.7 select_maximum_fusion.small_ref
  132.7 95.6 %reduce_all.1 = (bf16[4,1024,1024]{2,1,0:T(8,128)(2,1)}, f32[32,1024]{1,0:T(8,128)}) custom-call(bf16[2,128,1024]{2,1,0:T(8,128)(2,1)} %pad_maximum_fusion.1.left_ref, bf16[4,128,1024]{2,1,0:T(8,128)(2,1)} %pad_maximum_fusion.right_ref, f32[32,1024]{1,0:T(8,128)} %select_maximum_fusion.small_ref), custom_call_target="tpu_custom_call" | custom-call | tf_op jit(solution)/shard_map/reduce_all/pallas_call | solution.py:1014
  228.3 0.7 slice_reduce_fusion
  229.1 1.4 fusion.62
  230.5 1.5 slice_bitcast_fusion
  232.1 0.7 copy.51
  232.7 18.1 %finish.1 = (f32[1024,1024]{1,0:T(8,128)}, f32[1024,1024]{1,0:T(8,128)}, f32[1024,1024]{1,0:T(8,128)}, f32[1024,1024]{1,0:T(8,128)}, f32[2,704,1024]{2,1,0:T(8,1...) custom-call(bf16[4,1024,1024]{2,1,0:T(8,128)(2,1)} %get-tuple-element.46.sums_hbm, bf16[2,640,1024]{2,1,0:T(8,128)(2,1)} %bitcast.90, ...), custom_call_target="tpu_custom_call" | custom-call | tf_op jit(solution)/shard_map/finish/pallas_call | solution.py:764
  (56 shorter events, 4.2 us)
Async XLA Ops:
  105.0 2.1 copy-start.17
  107.1 5.9 %copy-start.1 = (f32[128,1024]{1,0:T(8,128)S(1)}, f32[128,1024]{1,0:T(8,128)}, u32[]{:S(2)}) copy-start(f32[128,1024]{1,0:T(8,128)} %get-tuple-element.36) | copy-start | bytes 1572868
  107.1 5.9 %copy-start.7 = (bf16[128,1024]{1,0:T(8,128)(2,1)S(1)}, bf16[128,1024]{1,0:T(8,128)(2,1)}, u32[]{:S(2)}) copy-start(bf16[128,1024]{1,0:T(8,128)(2,1)} %cot_ref.1) | copy-start | bytes 786436
  112.5 1.7 copy-start.14
  113.0 1.7 copy-start.11
  115.4 1.6 copy-start.2
  116.9 1.2 copy-start
  117.0 2.3 copy-start.12
  117.0 2.3 copy-start.13
  117.8 2.3 copy-start.8
  120.6 2.0 copy-start.10
  121.0 2.0 copy-start.9
  123.4 4.2 %copy-start.3 = (bf16[1024,1024]{1,0:T(8,128)(2,1)S(1)}, bf16[1024,1024]{1,0:T(8,128)(2,1)}, u32[]{:S(2)}) copy-start(bf16[1024,1024]{1,0:T(8,128)(2,1)} %wq_hbm.1) | copy-start | bytes 6291460
  125.2 3.3 %copy-start.5 = (bf16[1024,1024]{1,0:T(8,128)(2,1)S(1)}, bf16[1024,1024]{1,0:T(8,128)(2,1)}, u32[]{:S(2)}) copy-start(bf16[1024,1024]{1,0:T(8,128)(2,1)} %wk_hbm.1) | copy-start | bytes 6291460
  128.4 1.6 copy-start.4
  128.4 1.6 copy-start.6
  128.5 1.6 copy-start.15
  128.5 1.6 copy-start.16
where the time goes:
time: 256 us; the launch traced here: 251 us
  Pallas kernels  213 us (83%)
  local copies, waits for them, and re-layouts  16.5 us (6%)
  other arithmetic  10 us (4%)
  matrix products  9.93 us (4%)
    pallas_call x1, Pallas kernels, layer(): pl.pallas_call(functools.partial(layer_kernel, sizes, (micro, cap, per_co...  99.8 us
    pallas_call x1, Pallas kernels, reduce_all(): pl.pallas_call(functools.partial(reduce_kernel, sizes, pieces), out_shape...  95.6 us
    pallas_call x1, Pallas kernels, finish(): pl.pallas_call(finish_kernel, out_shape=(jax.ShapeDtypeStruct((width, wid...  18.1 us
    dot_general x11, matrix products, dot32(): return jnp.einsum(pattern, left, right, preferred_element_type=jnp.float32)  7.18 us
    pallas_call x3, local copies, waits for them, and re-layouts, layer(): pl.pallas_call(functools.partial(layer_kernel, sizes, (micro, cap, per_co...  5.44 us

commit v1 on v0

--- a/solution.py
+++ b/solution.py
@@ -774,15 +774,49 @@
     )(sums, x, h, dg, du, gr)
 
 
-def reduce_kernel(
-    sizes, pieces, left_ref, right_ref, small_ref, out_hbm, small_out,
-    out, sem_out, buf_a, buf_b, acc, *boxes,
+def upright(line):
+    n = line.shape[1]
+    square = lax.broadcasted_iota(jnp.int32, (n, n), 0) == lax.broadcasted_iota(jnp.int32, (n, n), 1)
+    return jnp.sum(jnp.where(square, jnp.broadcast_to(line, (n, n)), 0.0), axis=1, keepdims=True)
+
+
+def flat_line(column):
+    n = column.shape[0]
+    square = lax.broadcasted_iota(jnp.int32, (n, n), 0) == lax.broadcasted_iota(jnp.int32, (n, n), 1)
+    return jnp.sum(jnp.where(square, jnp.broadcast_to(column, (n, n)), 0.0), axis=0, keepdims=True)
+
+
+def diagonals(values):
+    n = values.shape[1]
+    total = None
+    for first in range(0, n, 8):
+        wide = jnp.concatenate([values[first : first + 8, :], jnp.zeros((8, n), jnp.float32)], axis=1)
+        wide = pltpu.roll(wide, n - first, 1)
+        total = wide if total is None else total + wide
+    row = lax.broadcasted_iota(jnp.int32, total.shape, 0)
+    for bit in (1, 2, 4):
+        total = jnp.where((row & bit) > 0, pltpu.roll(total, 2 * n - bit, 1), total)
+    return jnp.sum(total, axis=0, keepdims=True)
+
+
+def settle_kernel(
+    sizes, rows_per, pieces,
+    back_ref, info_ref, gate_ref, cot_ref, layer_in, residual, context, attn_in, query, key, value, probs,
+    norm_attn, norm_moe, router_t, wq_hbm, wk_hbm, wv_hbm, wo_hbm,
+    layer_out, grad_in, out_hbm, small_out,
+    weights, sem_a, left_ref, right_ref, small_ref, lines, out, sem_out, buf_a, buf_b, acc, *boxes,
 ):
+    bf, f32 = jnp.bfloat16, jnp.float32
+    micro, cap, per_core = rows_per
+    attn_w = []
+    for i, src in ((3, wo_hbm), (0, wq_hbm), (1, wk_hbm), (2, wv_hbm)):
+        attn_w.append(pltpu.make_async_copy(src, weights.at[i], sem_a.at[i]))
+        attn_w[-1].start()
     me = Place(*sizes)
     c, mate = me.c, me.at(c=1 - me.c)
     n = me.nx
     seq = right_ref.shape[1]
-    total_rows = out.shape[1]
+    total_rows = width = out.shape[1]
     is0 = c == 0
     pair = jnp.where(is0, me.x, me.y)
     other = jnp.where(is0, me.y, me.x)
@@ -814,6 +848,8 @@
     def slot_b(slot):
         return buf_b.at[pl.ds(pl.multiple_of(slot * seq, seq), seq), :]
 
+    left_ref[0] = attn_in[...]
+    left_ref[1] = context[...]
     targets = [
         (mate, 1 - c, other % 2, c),
         (me.at(x=flip_x, c=0), 0, flip_x % 2, 2 + c),
@@ -821,15 +857,119 @@
     ]
     factor = []
     for i, (device, role, parity, slot) in enumerate(targets):
-        a, b = jnp.where(role == 0, 0, parity), role * 2 + parity
+        a = jnp.where(role == 0, 0, parity)
         factor.append(remote(left_ref.at[a], slot_a(slot), fs.at[i, 0], fr.at[slot, 0], device))
-        factor.append(remote(right_ref.at[b], slot_b(slot), fs.at[i, 1], fr.at[slot, 1], device))
-    own = [
-        pltpu.make_async_copy(left_ref.at[jnp.where(is0, 0, lo)], slot_a(c), os.at[0]),
-        pltpu.make_async_copy(right_ref.at[c * 2 + lo], slot_b(c), os.at[1]),
-    ]
-    for copy in own:
-        copy.start()
+    own = [pltpu.make_async_copy(left_ref.at[jnp.where(is0, 0, lo)], slot_a(c), os.at[0])]
+    own[0].start()
+
+    size = 2 * per_core
+    group = lax.broadcasted_iota(jnp.int32, (1, seq), 1) // (seq // micro)
+    slot_ids = lax.broadcasted_iota(jnp.int32, (2 * me.n_expert * size, seq), 0)
+    hots = []
+    for k in range(2):
+        route, slot = info_ref[k : k + 1, :], info_ref[2 + k : 3 + k, :]
+        place = (route % 2) * (me.n_expert * size) + (route // 2) * size + c * per_core + group * cap + slot
+        hots.append(jnp.where(slot_ids == jnp.where(slot >= 0, place, -1), 1.0, 0.0))
+    low = [h.astype(bf) for h in hots] + [(hots[0] + hots[1]).astype(bf)]
+    half_slots = me.n_expert * size
+
+    def picked(hot, which):
+        total = None
+        for j in range(2):
+            rows = back_ref[which, j].reshape(half_slots, width)
+            term = dot_as(hot[j * half_slots : (j + 1) * half_slots, :], rows, TN)
+            total = term if total is None else total + term
+        return total
+
+    cot = cot_ref[...].astype(f32)
+    resid = residual[...]
+    chosen = [picked(low[k], 0) for k in range(2)]
+    gate = [upright(gate_ref[k : k + 1, :]) for k in range(2)]
+    layer_out[...] = (resid + (gate[0] * chosen[0] + gate[1] * chosen[1])).astype(bf)
+    grad_gate = [jnp.sum(cot * chosen[k], axis=-1, keepdims=True) for k in range(2)]
+    mean_grad = gate[0] * grad_gate[0] + gate[1] * grad_gate[1]
+    logit = [gate[k] * (grad_gate[k] - mean_grad) for k in range(2)]
+    experts = router_t.shape[0]
+    by_token, by_expert = None, None
+    for k in range(2):
+        route = info_ref[k : k + 1, :]
+        line = jnp.where(
+            lax.broadcasted_iota(jnp.int32, (experts, seq), 0) == route, flat_line(logit[k]), 0.0
+        )
+        by_expert = line if by_expert is None else by_expert + line
+        route_up = upright(route.astype(f32)).astype(jnp.int32)
+        line = jnp.where(
+            lax.broadcasted_iota(jnp.int32, (seq, experts), 1) == route_up, logit[k], 0.0
+        )
+        by_token = line if by_token is None else by_token + line
+
+    def exact(left, right):
+        return lax.dot_general(
+            left, right, (NN, ((), ())), preferred_element_type=f32, precision=highest
+        )
+
+    scale = row_scale(resid)
+    normed = resid * scale
+    small_ref[:experts] = exact(by_expert, normed * norm_moe[...])
+    grad_moe = picked(low[2], 1) + exact(by_token, router_t[...])
+    small_ref[experts:] = jnp.zeros((small_ref.shape[0] - experts, width), f32)
+    small_ref[experts + 1 : experts + 2] = jnp.sum(grad_moe * normed, axis=0, keepdims=True)
+    grad_n = grad_moe * norm_moe[...]
+    grad_resid = cot + scale * (grad_n - normed * jnp.mean(grad_n * normed, axis=-1, keepdims=True))
+    right_ref[3] = grad_resid.astype(bf)
+    grad_in[...] = grad_resid
+    attn_w[0].wait()
+    grad_context = dot_as(right_ref[3], weights[3], NT).astype(bf)
+
+    heads = probs.shape[0]
+    pair_lanes = 2 * width // heads
+    low_half = lax.broadcasted_iota(jnp.int32, (seq, pair_lanes), 1) < pair_lanes // 2
+    for n2 in range(heads // 2):
+        lanes = slice(n2 * pair_lanes, (n2 + 1) * pair_lanes)
+        sums = [None, None, None]
+        for h in range(2):
+            mine = low_half if h == 0 else ~low_half
+            head = 2 * n2 + h
+
+            def only(value):
+                return jnp.where(mine, value, jnp.zeros_like(value))
+
+            prob = probs[head]
+            grad_c = only(grad_context[:, lanes])
+            grad_p = dot_as(grad_c, value[:, lanes], NT)
+            grad_s = prob * (grad_p - jnp.sum(prob * grad_p, axis=-1, keepdims=True))
+            lines[head : head + 1, :] = diagonals(grad_s)
+            grad_s = grad_s.astype(bf)
+            terms = (
+                dot_as(grad_s, only(key[:, lanes]), NN),
+                dot_as(grad_s, only(query[:, lanes]), TN),
+                dot_as(prob.astype(bf), grad_c, TN),
+            )
+            sums = [t if s is None else s + t for s, t in zip(sums, terms)]
+        for i in range(3):
+            right_ref[i, :, lanes] = sums[i].astype(bf)
+    for i, (device, role, parity, slot) in enumerate(targets):
+        factor.append(
+            remote(right_ref.at[role * 2 + parity], slot_b(slot), fs.at[i, 1], fr.at[slot, 1], device)
+        )
+    own.append(pltpu.make_async_copy(right_ref.at[c * 2 + lo], slot_b(c), os.at[1]))
+    own[1].start()
+    buckets = 32
+    bucket = bucket_of(lax.broadcasted_iota(jnp.int32, (2 * seq, buckets), 0) - seq)
+    hot = jnp.where(bucket == lax.broadcasted_iota(jnp.int32, (2 * seq, buckets), 1), 1.0, 0.0)
+    small_ref[experts + 8 : experts + 8 + heads, :buckets] = exact(lines[...], hot)
+    grad_attn = None
+    for i in range(3):
+        attn_w[1 + i].wait()
+        term = dot_as(right_ref[i], weights[i], NT)
+        grad_attn = term if grad_attn is None else grad_attn + term
+    rows = layer_in[...].astype(f32)
+    scale = row_scale(rows)
+    normed = rows * scale
+    small_ref[experts : experts + 1] = jnp.sum(grad_attn * normed, axis=0, keepdims=True)
+    grad_n = grad_attn * norm_attn[...]
+    grad_in[...] += scale * (grad_n - normed * jnp.mean(grad_n * normed, axis=-1, keepdims=True))
+
     rows_s = half.shape[0]
     small = [remote(small_ref.at[pl.ds((1 - c) * rows_s, rows_s)], half, ss.at[0], sr.at[0], mate)]
     small_dims = [
@@ -885,7 +1025,7 @@
 
     def multiply(k):
         acc[k] = lax.dot_general(
-            buf_a[:, k * rows_k : (k + 1) * rows_k], buf_b[...], (((0,), (0,)), ((), ())),
+            buf_a[:, k * rows_k : (k + 1) * rows_k], buf_b[...], (TN, ((), ())),
             preferred_element_type=jnp.float32,
         )
         push(k, 0, rows_k)
@@ -897,7 +1037,7 @@
         copies = []
         for s in range(1, count):
             to = (index + s) % count
-            parts[level][k, s - 1] = acc[k, pl.ds(pl.multiple_of(to * size, 8), size), :].astype(jnp.bfloat16)
+            parts[level][k, s - 1] = acc[k, pl.ds(pl.multiple_of(to * size, 16), size), :].astype(jnp.bfloat16)
             copies.append(
                 remote(
                     parts[level].at[k, s - 1], gots[level].at[k, s - 1],
@@ -918,7 +1058,7 @@
         size = rows_at(at) // count
         for copy in pending["push", at, k]:
             copy.wait_recv()
-        total = acc[k, pl.ds(pl.multiple_of(index * size, 8), size), :]
+        total = acc[k, pl.ds(pl.multiple_of(index * size, 16), size), :]
         for s in range(1, count):
             total = total + gots[level][k, s - 1].astype(jnp.float32)
         if at + 1 < len(levels):
@@ -934,7 +1074,7 @@
             count, index, _ = dims[levels[i]]
             rows //= count
             start = start + index * rows
-        return pl.multiple_of(start, 8)
+        return pl.multiple_of(start, 16)
 
     def share(k, at):
         level = levels[at]
@@ -995,31 +1135,46 @@
         copy.wait()
 
 
-def reduce_all(sizes, left, right, small, pieces=8):
+def settle(sizes, micro, cap, arrays, norms, router_t, attn_w):
     n_expert, n_dp = sizes
     nz = math.gcd(n_expert, 4)
     n = n_expert // nz
     nh = n // 2
     assert n == n_dp // 2
-    seq, width = left.shape[1:]
+    seq, width = arrays[4].shape
+    heads = arrays[11].shape[0]
+    splits = [n, nh, 2, nz // 2]
+    pieces = max(1, min(8, width // (16 * math.prod(splits))))
     rows_k = width // pieces
     bf, f32 = jnp.bfloat16, jnp.float32
-    rows_s = small.shape[0] // 2
-    splits = [n, nh, 2, nz // 2]
+    small_rows = router_t.shape[0] + 8 + heads
+    small_rows += -small_rows % 16
+    rows_s = small_rows // 2
     sizes_at = [rows_k // math.prod(splits[: i + 1]) for i in range(4)]
     counts = [max(q - 1, 1) for q in splits]
     most = max(counts)
-    boxes = [pltpu.VMEM((pieces, q, s, width), bf) for q, s in zip(counts, sizes_at)]
+    boxes = [
+        pltpu.VMEM((pieces, q, s if k > 1 else 16, width), bf) for q, s, k in zip(counts, sizes_at, splits)
+    ]
     smalls = 2 * n + nz
+    any_space = pl.BlockSpec(memory_space=pl.ANY)
     return pl.pallas_call(
-        functools.partial(reduce_kernel, sizes, pieces),
+        functools.partial(settle_kernel, sizes, (micro, cap, micro * cap), pieces),
         out_shape=(
+            jax.ShapeDtypeStruct((seq, width), bf),
+            jax.ShapeDtypeStruct((seq, width), f32),
             jax.ShapeDtypeStruct((4, width, width), bf),
-            jax.ShapeDtypeStruct(small.shape, f32),
+            jax.ShapeDtypeStruct((small_rows, width), f32),
         ),
-        in_specs=[VMEM] * 3,
-        out_specs=(pl.BlockSpec(memory_space=pl.ANY), VMEM),
+        in_specs=[VMEM] * 15 + [any_space] * 4,
+        out_specs=(VMEM, VMEM, any_space, VMEM),
         scratch_shapes=[
+            pltpu.VMEM((4, width, width), bf),
+            DMA((4,)),
+            pltpu.VMEM((2, seq, width), bf),
+            pltpu.VMEM((4, seq, width), bf),
+            pltpu.VMEM((small_rows, width), f32),
+            pltpu.VMEM((heads, 2 * seq), f32),
             pltpu.VMEM((4, width, width), bf),
             DMA((2, pieces)),
             pltpu.VMEM((4 * seq, width), bf),
@@ -1044,11 +1199,11 @@
             DMA((smalls,)),
             DMA((smalls,)),
         ],
-        name="reduce_all",
+        name="settle",
         compiler_params=pltpu.CompilerParams(
-            collective_id=3, has_side_effects=True, vmem_limit_bytes=56 << 20
+            collective_id=3, has_side_effects=True, vmem_limit_bytes=58 << 20
         ),
-    )(left, right, small)
+    )(*arrays, *norms, router_t, *attn_w)
 
 
 def rms_scale(values):
@@ -1057,13 +1212,8 @@
 
 def bucket_hot(seq_len, buckets):
     position = jnp.arange(seq_len, dtype=jnp.int32)
-    relative = position[None, :] - position[:, None]
-    distance = jnp.abs(relative)
-    far_bucket = jnp.full_like(distance, 8)
-    for threshold in bucket_edges:
-        far_bucket = far_bucket + (distance >= threshold).astype(jnp.int32)
-    bucketed = jnp.where(distance < 8, distance, far_bucket) + 16 * (relative > 0).astype(jnp.int32)
     bucket_ids = jnp.arange(buckets, dtype=jnp.int32)
+    bucketed = bucket_of(position[None, :] - position[:, None])
     return (bucketed[None, :, :] == bucket_ids[:, None, None]).astype(jnp.float32)
 
 
@@ -1085,10 +1235,6 @@
     group_len = seq_len // MICRO
     capacity = (5 * group_len + 2 * expert_count - 1) // (2 * expert_count)
     split_heads = (seq_len, heads, width // heads)
-    layer_rows = layer_in.astype(f32)
-    inv_attn = rms_scale(layer_rows)
-    normed_attn = layer_rows * inv_attn
-    one_hot = bucket_hot(seq_len, buckets)
     info = jnp.concatenate([routes.T, queue_slots.T, jnp.zeros((4, seq_len), jnp.int32)])
     expert_w = [jnp.swapaxes(w_gate, 1, 2), jnp.swapaxes(w_up, 1, 2), w_down]
     slots = n_dp // 2 * n_expert * 2 * MICRO * capacity
@@ -1102,10 +1248,12 @@
             info, cotangent, (w_query, w_key, w_value, w_out), expert_w,
         )
     else:
-        attn_in = (normed_attn * norm_attn).astype(bf)
+        layer_rows = layer_in.astype(f32)
+        attn_in = (layer_rows * rms_scale(layer_rows) * norm_attn).astype(bf)
         query = dot32("sd,de->se", attn_in, w_query).astype(bf)
         key = dot32("sd,de->se", attn_in, w_key).astype(bf)
         value = dot32("sd,de->se", attn_in, w_value).astype(bf)
+        one_hot = bucket_hot(seq_len, buckets)
         bias = jnp.einsum("bij,bh->hij", one_hot, rel_table, precision=highest)
         scores = dot32("ihd,jhd->hij", query.reshape(split_heads), key.reshape(split_heads)) + bias
         exponent = jnp.exp(scores - jnp.max(scores, axis=-1, keepdims=True))
@@ -1113,13 +1261,10 @@
         context = dot32("hij,jhd->ihd", probs.astype(bf), value.reshape(split_heads))
         context = context.astype(bf).reshape(seq_len, width)
         residual = layer_rows + dot32("se,ed->sd", context, w_out)
-    inv_moe = rms_scale(residual)
-    normed_moe = residual * inv_moe
-    moe_in = normed_moe * norm_moe
-    expert_ids = jnp.arange(expert_count, dtype=jnp.int32)
-    first_hot = (routes[:, 0:1] == expert_ids).astype(f32)
-    second_hot = (routes[:, 1:2] == expert_ids).astype(f32)
-    if not fused:
+        moe_in = residual * rms_scale(residual) * norm_moe
+        expert_ids = jnp.arange(expert_count, dtype=jnp.int32)
+        first_hot = (routes[:, 0:1] == expert_ids).astype(f32)
+        second_hot = (routes[:, 1:2] == expert_ids).astype(f32)
         gate_prob = jax.nn.softmax(jnp.dot(moe_in, router, precision=highest), axis=-1)
         prob_first, prob_second = jnp.sum(gate_prob * first_hot, axis=-1), jnp.sum(gate_prob * second_hot, axis=-1)
         gates = jnp.stack([prob_first, prob_second]) / (prob_first + prob_second)
@@ -1140,84 +1285,22 @@
         gate_grad, up_grad = (hidden_grad * lean).astype(bf), (hidden_grad * active).astype(bf)
         rows_grad = dot32("jrf,jdf->jrd", gate_grad, w_gate) + dot32("jrf,jdf->jrd", up_grad, w_up)
         back = gather_back(sizes, partial_out.reshape(blocks), rows_grad.astype(bf).reshape(blocks))
-    weight_first, weight_second = gates[0][:, None], gates[1][:, None]
-    query_heads, key_heads, value_heads = [a.reshape(split_heads) for a in (query, key, value)]
-    probs_low = probs.astype(bf)
+    layer_out, grad_input, sums, small = settle(
+        sizes, MICRO, capacity,
+        (back, info, gates, cotangent, layer_in, residual, context, attn_in, query, key, value, probs),
+        (norm_attn[None], norm_moe[None]), router.T, (w_query, w_key, w_value, w_out),
+    )
     rows_in, hidden, gate_grad, up_grad, grad_rows = [
         a.reshape(2, -1, a.shape[-1]) for a in (rows_in, hidden, gate_grad, up_grad, grad_rows)
     ]
-    back = back.reshape(2, -1, width)
-
-    core = lax.axis_index("dp") % 2
-    per_core = MICRO * capacity
-    token = jnp.arange(seq_len, dtype=jnp.int32)[:, None]
-    place = (routes % 2) * (n_expert * 2 * per_core) + (routes // 2) * (2 * per_core)
-    place = place + core * per_core + (token // group_len) * capacity + queue_slots
-    place = jnp.where(queue_slots >= 0, place, -1)
-    slot_ids = jnp.arange(2 * n_expert * 2 * per_core, dtype=jnp.int32)
-    select_first = (place[:, 0:1] == slot_ids).astype(bf)
-    select_second = (place[:, 1:2] == slot_ids).astype(bf)
-    picked_first = dot32("tp,pd->td", select_first, back[0])
-    picked_second = dot32("tp,pd->td", select_second, back[0])
-    moe = weight_first * picked_first + weight_second * picked_second
-    layer_out = (residual + moe).astype(bf)
-    cot_rows = cotangent.astype(f32)
-    grad_weight_first = jnp.sum(cot_rows * picked_first, axis=-1, keepdims=True)
-    grad_weight_second = jnp.sum(cot_rows * picked_second, axis=-1, keepdims=True)
-    grad_from_slots = dot32("tp,pd->td", select_first + select_second, back[1])
-    mean_grad = weight_first * grad_weight_first + weight_second * grad_weight_second
-    logit_first = weight_first * (grad_weight_first - mean_grad)
-    logit_second = weight_second * (grad_weight_second - mean_grad)
-    grad_logits = logit_first * first_hot + logit_second * second_hot
-    grad_router = jnp.einsum("sd,se->ed", moe_in, grad_logits, precision=highest)
-    grad_moe_in = grad_from_slots + jnp.einsum("se,de->sd", grad_logits, router, precision=highest)
-    grad_norm_moe = jnp.sum(grad_moe_in * normed_moe, axis=0)
-    grad_normed = grad_moe_in * norm_moe
-    grad_residual = cot_rows + inv_moe * (
-        grad_normed - normed_moe * jnp.mean(grad_normed * normed_moe, axis=-1, keepdims=True)
-    )
-    grad_attn_low = grad_residual.astype(bf)
-    grad_context = dot32("sd,ed->se", grad_attn_low, w_out).astype(bf).reshape(split_heads)
-    grad_values = dot32("hij,ihd->jhd", probs_low, grad_context).astype(bf).reshape(seq_len, width)
-    grad_probs = dot32("ihd,jhd->hij", grad_context, value_heads)
-    grad_scores = probs * (grad_probs - jnp.sum(probs * grad_probs, axis=-1, keepdims=True))
-    grad_rel_table = jnp.einsum("bij,hij->bh", one_hot, grad_scores, precision=highest)
-    scores_low = grad_scores.astype(bf)
-    grad_queries = dot32("hij,jhd->ihd", scores_low, key_heads).astype(bf).reshape(seq_len, width)
-    grad_keys = dot32("hij,ihd->jhd", scores_low, query_heads).astype(bf).reshape(seq_len, width)
-    grad_attn_in = dot32("se,de->sd", grad_queries, w_query)
-    grad_attn_in = grad_attn_in + dot32("se,de->sd", grad_keys, w_key)
-    grad_attn_in = grad_attn_in + dot32("se,de->sd", grad_values, w_value)
-    grad_norm_attn = jnp.sum(grad_attn_in * normed_attn, axis=0)
-    grad_normed_attn = grad_attn_in * norm_attn
-    grad_input = grad_residual + inv_attn * (
-        grad_normed_attn
-        - normed_attn * jnp.mean(grad_normed_attn * normed_attn, axis=-1, keepdims=True)
-    )
-    table = grad_rel_table.reshape(-1)
-    small = jnp.concatenate(
-        [
-            grad_router,
-            grad_norm_attn[None],
-            grad_norm_moe[None],
-            jnp.pad(table, (0, width - table.size))[None],
-        ]
-    )
-    small = jnp.pad(small, ((0, -small.shape[0] % 16), (0, 0)))
-    sums, small = reduce_all(
-        sizes,
-        jnp.stack([attn_in, context]),
-        jnp.stack([grad_queries, grad_keys, grad_values, grad_attn_low]),
-        small,
-    )
     *matrices, grad_w_gate, grad_w_up, grad_w_down = finish(
         sums, rows_in, hidden, gate_grad, up_grad, grad_rows
     )
-    grad_w_gate, grad_w_up = jnp.swapaxes(grad_w_gate, 1, 2), jnp.swapaxes(grad_w_up, 1, 2)
     return (
         layer_out, grad_input, small[expert_count], *matrices,
-        small[expert_count + 2, : table.size].reshape(buckets, heads),
-        small[expert_count + 1], small[:expert_count].T, grad_w_gate, grad_w_up, grad_w_down,
+        small[expert_count + 8 : expert_count + 8 + heads, :buckets].T,
+        small[expert_count + 1], small[:expert_count].T,
+        jnp.swapaxes(grad_w_gate, 1, 2), jnp.swapaxes(grad_w_up, 1, 2), grad_w_down,
     )
 
 

time: 256 us -> 228 us (0.89); the launches traced: 251 us -> 228 us
  local copies, waits for them, and re-layouts: 16.5 us -> 5.79 us
  matrix products: 9.93 us -> 0 us
  other arithmetic: 10 us -> 1.36 us
  Pallas kernels: 213 us -> 220 us
    dot_general x14 -> x0, matrix products: 9.93 us -> none  [the longest x11 7.18 us: dot32(): return jnp.einsum(pattern, left, right, preferred_element_type=jnp.float32)]
    pallas_call x1, Pallas kernels: 95.6 us -> 102 us  [settle(): pl.pallas_call(functools.partial(settle_kernel, sizes, (micro, cap, micro...]
    pallas_call x3 -> x0, local copies, waits for them, and re-layouts: 5.44 us -> none  [layer(): pl.pallas_call(functools.partial(layer_kernel, sizes, (micro, cap, per_co...]
    another operation x3 -> x0, other arithmetic: 4.19 us -> none  [the longest x2 3.35 us: shards(): jnp.stack([grad_queries, grad_keys, grad_values, grad_attn_low])]
    slice x2 -> x0, local copies, waits for them, and re-layouts: 2.75 us -> none  [the longest x1 2.01 us: shards(): grad_from_slots = dot32('tp,pd->td', select_first + select_second, back[1])]
    another operation x4 -> x0, local copies, waits for them, and re-layouts: 2.63 us -> none  [the longest x3 2.55 us: shards(): jnp.stack([grad_queries, grad_keys, grad_values, grad_attn_low])]
where the time goes in v1:
time: 228 us
  Pallas kernels  220 us (96%)
  local copies, waits for them, and re-layouts  5.79 us (3%)
    pallas_call x1, Pallas kernels, settle(): pl.pallas_call(functools.partial(settle_kernel, sizes, (micro, cap, micro...  102 us
    pallas_call x1, Pallas kernels, layer(): pl.pallas_call(functools.partial(layer_kernel, sizes, (micro, cap, per_co...  99.4 us
    pallas_call x1, Pallas kernels, finish(): pl.pallas_call(finish_kernel, out_shape=(jax.ShapeDtypeStruct((width, wid...  18.3 us

profile of v1, /device:TPU:1, one launch (start us, length us, event | category | flops | bytes accessed | tf_op | source)
XLA Modules:
  0.0 227.8 jit_solution(13148065200524625259)
XLA Ops:
  0.7 0.1 pad.2.clone
  0.7 1.4 add_add_fusion.info_ref
  2.1 99.4 %layer.1 = (bf16[2,2,8,40,1024]{4,3,2,1,0:T(8,128)(2,1)}, bf16[2,16,40,1024]{3,2,1,0:T(8,128)(2,1)}, bf16[2,16,40,704]{3,2,1,0:T(8,128)(2,1)}, bf16[2,16,40,704]...) custom-call(bf16[128,1024]{1,0:T(8,128)(2,1)} %layer_in.3, ...), custom_call_target="tpu_custom_call" | custom-call | tf_op jit(solution)/shard_map/layer/pallas_call | solution.py:660
  101.5 102.2 %settle.1 = (bf16[128,1024]{1,0:T(8,128)(2,1)}, f32[128,1024]{1,0:T(8,128)}, bf16[4,1024,1024]{2,1,0:T(8,128)(2,1)}, f32[48,1024]{1,0:T(8,128)}) custom-call(bf16[2,2,8,40,1024]{4,3,2,1,0:T(8,128)(2,1)} %get-tuple-element.38.back_ref, s32[8,128]{1,0:T(8,128)} %add_add_fusion.info_ref, f32[8,128]{1,0:T(8,128)} %get-tuple-element.39.gate_ref, ...), custom_call_target="tpu_custom_call" | custom-call | tf_op jit(solution)/shard_map/settle/pallas_call | solution.py:1161
  203.8 1.3 slice_bitcast_fusion.1
  205.1 1.4 fusion
  206.5 1.5 slice_bitcast_fusion
  208.0 0.0 copy-start.1
  208.0 0.0 copy-start
  208.0 18.3 %finish.1 = (f32[1024,1024]{1,0:T(8,128)}, f32[1024,1024]{1,0:T(8,128)}, f32[1024,1024]{1,0:T(8,128)}, f32[1024,1024]{1,0:T(8,128)}, f32[2,704,1024]{2,1,0:T(8,1...) custom-call(bf16[4,1024,1024]{2,1,0:T(8,128)(2,1)} %get-tuple-element.50.sums_hbm, bf16[2,640,1024]{2,1,0:T(8,128)(2,1)} %bitcast.23, ...), custom_call_target="tpu_custom_call" | custom-call | tf_op jit(solution)/shard_map/finish/pallas_call | solution.py:764
  226.3 0.0 copy-done.1
  226.3 0.7 copy.30
  227.0 0.0 copy-done
  227.0 0.8 copy.31
  (1 shorter events, 0.0 us)
Async XLA Ops:
  208.0 18.3 %copy-start.1 = (bf16[128,1024]{1,0:T(8,128)(2,1)S(1)}, bf16[128,1024]{1,0:T(8,128)(2,1)}, u32[]{:S(2)}) copy-start(bf16[128,1024]{1,0:T(8,128)(2,1)} %get-tuple-element.78) | copy-start | bytes 786436
  208.0 19.1 %copy-start = (f32[128,1024]{1,0:T(8,128)S(1)}, f32[128,1024]{1,0:T(8,128)}, u32[]{:S(2)}) copy-start(f32[128,1024]{1,0:T(8,128)} %get-tuple-element.79) | copy-start | bytes 1572868

commit v2 on v1

--- a/solution.py
+++ b/solution.py
@@ -426,10 +426,11 @@
 
 
 def layer_kernel(
-    sizes, rows_per, layer_in, norm_attn, norm_moe, table_t, router_t, info_ref, cot_ref,
+    sizes, rows_per, layer_in, norm_attn, norm_moe, table_t, router_t, route_ref, slot_ref, cot_ref,
     wq_hbm, wk_hbm, wv_hbm, wo_hbm, wg_hbm, wu_hbm, wd_hbm,
-    q_out, x_ref, hid_out, dg_out, du_out, gr_out, query, key, value, probs, context, residual, attn_in, gate_out,
-    g_ref, w_ref, weights, act, slope, away, own, sem_a, sem_w, *scratch,
+    q_out, x_hbm, hid_hbm, dg_hbm, du_hbm, gr_hbm, query, key, value, probs, context, residual, attn_in, gate_out,
+    x_ref, hid_out, dg_out, du_out, gr_out, g_ref, w_ref, weights, act, slope, away, own,
+    sem_a, sem_w, sem_e, *scratch,
 ):
     me = Place(*sizes)
     c = me.c
@@ -454,7 +455,9 @@
     scratch = scratch[14:]
     column = me.n_expert
     quarter = [range(i * column // 4, (i + 1) * column // 4) for i in range(4)]
-    info_all[c] = info_ref[...]
+    info_all[c, 0:2, :] = route_ref[...]
+    info_all[c, 2:4, :] = slot_ref[...]
+    info_all[c, 4:, :] = jnp.zeros((4, seq), jnp.int32)
     rows_in.share("info", info_all)
     tok[1, c] = cot_ref[...]
     rows_in.share(1, tok.at[1])
@@ -510,7 +513,7 @@
     gate_prob = logits / jnp.sum(logits, axis=0, keepdims=True)
     expert_ids = lax.broadcasted_iota(jnp.int32, gate_prob.shape, 0)
     picked = [
-        jnp.sum(jnp.where(info_ref[k : k + 1, :] == expert_ids, gate_prob, 0.0), axis=0, keepdims=True)
+        jnp.sum(jnp.where(route_ref[k : k + 1, :] == expert_ids, gate_prob, 0.0), axis=0, keepdims=True)
         for k in range(2)
     ]
     both = picked[0] + picked[1]
@@ -536,6 +539,11 @@
         lambda i, block: own[i, pl.ds(pl.multiple_of(block * size, 8), size), :],
         q_out, *scratch[:4], scratch[4:],
     )
+
+    def emit(i, src, dst):
+        copy = pltpu.make_async_copy(src, dst, sem_e.at[i])
+        copy.start()
+        return copy
 
     def part(i, j):
         return weights[pl.ds(pl.multiple_of((2 * i + j) * units, 16), units), :]
@@ -636,17 +644,21 @@
     back.to_mate(1, 0)
     back.finish(0, shares[2])
     backward(False, c, here, column)
+    saved = ((x_ref, x_hbm), (hid_out, hid_hbm), (dg_out, dg_hbm), (du_out, du_hbm), (gr_out, gr_hbm))
+    copies = [emit(i, src, dst) for i, (src, dst) in enumerate(saved)]
     back.finish(0, shares[3])
     back.across(0)
     back.finish(1, back.order)
     back.across(1)
     back.close()
+    for copy in copies:
+        copy.wait()
     for payload in (out_x, out_w, out_g):
         payload.close()
     rows_in.close()
 
 
-def layer(sizes, micro, cap, layer_in, norms, table_t, router_t, info, cot, attn_w, expert_w):
+def layer(sizes, micro, cap, layer_in, norms, table_t, router_t, places, cot, attn_w, expert_w):
     n_expert, ny, per_core = sizes[0], sizes[1] // 2, micro * cap
     seq, width = cot.shape
     units = expert_w[0].shape[1]
@@ -664,9 +676,14 @@
             low, low, low, jax.ShapeDtypeStruct((heads, seq, seq), f32), low, full, low,
             jax.ShapeDtypeStruct((8, seq), f32),
         ),
-        in_specs=[VMEM] * 7 + [any_space] * 7,
-        out_specs=(VMEM,) * 14,
+        in_specs=[VMEM] * 8 + [any_space] * 7,
+        out_specs=(VMEM,) + (any_space,) * 5 + (VMEM,) * 8,
         scratch_shapes=[
+            pltpu.VMEM(outer.shape, bf),
+            pltpu.VMEM(inner.shape, bf),
+            pltpu.VMEM(inner.shape, bf),
+            pltpu.VMEM(inner.shape, bf),
+            pltpu.VMEM(outer.shape, bf),
             pltpu.VMEM((2, count, size, width), bf),
             pltpu.VMEM((2, count, 8, 128), f32),
             pltpu.VMEM((max(4 * width, 6 * units), width), bf),
@@ -676,19 +693,21 @@
             pltpu.VMEM((2, count * size, width), f32),
             DMA((4,)),
             DMA((2, 3)),
+            DMA((5,)),
         ]
         + rows_scratch(sizes, per_core, seq, width)
         + spread_sems(sizes)
         + back_scratch(sizes, size, width),
         name="layer",
         compiler_params=pltpu.CompilerParams(
-            collective_id=4, has_side_effects=True, vmem_limit_bytes=54 << 20
+            collective_id=4, has_side_effects=True, vmem_limit_bytes=60 << 20
         ),
-    )(layer_in, *norms, table_t, router_t, info, cot, *attn_w, *expert_w)
-
-
-def finish_kernel(sums_hbm, x_hbm, h_hbm, dg_hbm, du_hbm, gr_hbm, *refs):
-    outs, (sums, x, h, dg, du, gr, stage, sem_sum, sem_in, sem_out) = refs[:7], refs[7:]
+    )(layer_in, *norms, table_t, router_t, *places, cot, *attn_w, *expert_w)
+
+
+def finish_kernel(small, sums_hbm, x_hbm, h_hbm, dg_hbm, du_hbm, gr_hbm, *refs):
+    outs, (router_out, attn_out, moe_out, table_out) = refs[:7], refs[7:11]
+    sums, x, h, dg, du, gr, stage, sem_sum, sem_in, sem_out = refs[11:]
     slots, rows = stage.shape[:2]
     width = sums.shape[1]
     units = h.shape[2]
@@ -711,6 +730,11 @@
         for j in range(2):
             load((key, j), src.at[j], dst.at[j], sem_in.at[i, j])
     load_sums(casts[4:])
+    experts = router_out.shape[0]
+    router_out[...] = small[:experts]
+    attn_out[...] = small[experts : experts + 1]
+    moe_out[...] = small[experts + 1 : experts + 2]
+    table_out[...] = small[experts + 8 : experts + 8 + table_out.shape[0], : table_out.shape[1]]
 
     def need(key):
         if key in loads:
@@ -756,7 +780,7 @@
             copy.wait()
 
 
-def finish(sums, x, h, dg, du, gr):
+def finish(sums, small, x, h, dg, du, gr, experts, table):
     f32 = jnp.float32
     width = sums.shape[1]
     units = h.shape[2]
@@ -764,14 +788,15 @@
     return pl.pallas_call(
         finish_kernel,
         out_shape=(jax.ShapeDtypeStruct((width, width), f32),) * 4
-        + (jax.ShapeDtypeStruct((2, units, width), f32),) * 3,
-        in_specs=[any_space] * 6,
-        out_specs=(any_space,) * 7,
+        + (jax.ShapeDtypeStruct((2, units, width), f32),) * 3
+        + tuple(jax.ShapeDtypeStruct(a, f32) for a in ((experts, width), (1, width), (1, width), table)),
+        in_specs=[VMEM] + [any_space] * 6,
+        out_specs=(any_space,) * 7 + (VMEM,) * 4,
         scratch_shapes=[pltpu.VMEM(a.shape, a.dtype) for a in (sums, x, h, dg, du, gr)]
         + [pltpu.VMEM((6, 256, width), f32), DMA((4 * width // 256,)), DMA((5, 2)), DMA((6,))],
         name="finish",
         compiler_params=pltpu.CompilerParams(vmem_limit_bytes=60 << 20),
-    )(sums, x, h, dg, du, gr)
+    )(small, sums, x, h, dg, du, gr)
 
 
 def upright(line):
@@ -801,7 +826,7 @@
 
 def settle_kernel(
     sizes, rows_per, pieces,
-    back_ref, info_ref, gate_ref, cot_ref, layer_in, residual, context, attn_in, query, key, value, probs,
+    back_ref, route_ref, slot_ref, gate_ref, cot_ref, layer_in, residual, context, attn_in, query, key, value, probs,
     norm_attn, norm_moe, router_t, wq_hbm, wk_hbm, wv_hbm, wo_hbm,
     layer_out, grad_in, out_hbm, small_out,
     weights, sem_a, left_ref, right_ref, small_ref, lines, out, sem_out, buf_a, buf_b, acc, *boxes,
@@ -867,7 +892,7 @@
     slot_ids = lax.broadcasted_iota(jnp.int32, (2 * me.n_expert * size, seq), 0)
     hots = []
     for k in range(2):
-        route, slot = info_ref[k : k + 1, :], info_ref[2 + k : 3 + k, :]
+        route, slot = route_ref[k : k + 1, :], slot_ref[k : k + 1, :]
         place = (route % 2) * (me.n_expert * size) + (route // 2) * size + c * per_core + group * cap + slot
         hots.append(jnp.where(slot_ids == jnp.where(slot >= 0, place, -1), 1.0, 0.0))
     low = [h.astype(bf) for h in hots] + [(hots[0] + hots[1]).astype(bf)]
@@ -892,7 +917,7 @@
     experts = router_t.shape[0]
     by_token, by_expert = None, None
     for k in range(2):
-        route = info_ref[k : k + 1, :]
+        route = route_ref[k : k + 1, :]
         line = jnp.where(
             lax.broadcasted_iota(jnp.int32, (experts, seq), 0) == route, flat_line(logit[k]), 0.0
         )
@@ -1141,8 +1166,8 @@
     n = n_expert // nz
     nh = n // 2
     assert n == n_dp // 2
-    seq, width = arrays[4].shape
-    heads = arrays[11].shape[0]
+    seq, width = arrays[5].shape
+    heads = arrays[12].shape[0]
     splits = [n, nh, 2, nz // 2]
     pieces = max(1, min(8, width // (16 * math.prod(splits))))
     rows_k = width // pieces
@@ -1166,7 +1191,7 @@
             jax.ShapeDtypeStruct((4, width, width), bf),
             jax.ShapeDtypeStruct((small_rows, width), f32),
         ),
-        in_specs=[VMEM] * 15 + [any_space] * 4,
+        in_specs=[VMEM] * 16 + [any_space] * 4,
         out_specs=(VMEM, VMEM, any_space, VMEM),
         scratch_shapes=[
             pltpu.VMEM((4, width, width), bf),
@@ -1235,7 +1260,7 @@
     group_len = seq_len // MICRO
     capacity = (5 * group_len + 2 * expert_count - 1) // (2 * expert_count)
     split_heads = (seq_len, heads, width // heads)
-    info = jnp.concatenate([routes.T, queue_slots.T, jnp.zeros((4, seq_len), jnp.int32)])
+    places = (routes.T, queue_slots.T)
     expert_w = [jnp.swapaxes(w_gate, 1, 2), jnp.swapaxes(w_up, 1, 2), w_down]
     slots = n_dp // 2 * n_expert * 2 * MICRO * capacity
     fused = 2 * slots * width * 20 + 6 * w_gate.size < 52 << 20
@@ -1245,7 +1270,7 @@
             query, key, value, probs, context, residual, attn_in, gates,
         ) = layer(
             sizes, MICRO, capacity, layer_in, (norm_attn[None], norm_moe[None]), rel_table.T, router.T,
-            info, cotangent, (w_query, w_key, w_value, w_out), expert_w,
+            places, cotangent, (w_query, w_key, w_value, w_out), expert_w,
         )
     else:
         layer_rows = layer_in.astype(f32)
@@ -1269,6 +1294,7 @@
         prob_first, prob_second = jnp.sum(gate_prob * first_hot, axis=-1), jnp.sum(gate_prob * second_hot, axis=-1)
         gates = jnp.stack([prob_first, prob_second]) / (prob_first + prob_second)
         gates = jnp.pad(gates, ((0, 6), (0, 0)))
+        info = jnp.concatenate([*places, jnp.zeros((4, seq_len), jnp.int32)])
         rows_in, weight_in, grad_in = spread(
             sizes, MICRO, capacity, info, moe_in.astype(bf), cotangent, gates
         )
@@ -1287,19 +1313,21 @@
         back = gather_back(sizes, partial_out.reshape(blocks), rows_grad.astype(bf).reshape(blocks))
     layer_out, grad_input, sums, small = settle(
         sizes, MICRO, capacity,
-        (back, info, gates, cotangent, layer_in, residual, context, attn_in, query, key, value, probs),
+        (back, *places, gates, cotangent, layer_in, residual, context, attn_in, query, key, value, probs),
         (norm_attn[None], norm_moe[None]), router.T, (w_query, w_key, w_value, w_out),
     )
     rows_in, hidden, gate_grad, up_grad, grad_rows = [
         a.reshape(2, -1, a.shape[-1]) for a in (rows_in, hidden, gate_grad, up_grad, grad_rows)
     ]
-    *matrices, grad_w_gate, grad_w_up, grad_w_down = finish(
-        sums, rows_in, hidden, gate_grad, up_grad, grad_rows
+    (
+        *matrices, grad_w_gate, grad_w_up, grad_w_down,
+        grad_router, grad_norm_attn, grad_norm_moe, grad_table,
+    ) = finish(
+        sums, small, rows_in, hidden, gate_grad, up_grad, grad_rows, expert_count, (heads, buckets)
     )
     return (
-        layer_out, grad_input, small[expert_count], *matrices,
-        small[expert_count + 8 : expert_count + 8 + heads, :buckets].T,
-        small[expert_count + 1], small[:expert_count].T,
+        layer_out, grad_input, grad_norm_attn.reshape(width), *matrices, grad_table.T,
+        grad_norm_moe.reshape(width), grad_router.T,
         jnp.swapaxes(grad_w_gate, 1, 2), jnp.swapaxes(grad_w_up, 1, 2), grad_w_down,
     )
 

time: 228 us -> 221 us (0.969)
  local copies, waits for them, and re-layouts: 5.79 us -> 1.51 us
    pallas_call x1, Pallas kernels: 99.4 us -> 96.4 us  [layer(): pl.pallas_call(functools.partial(layer_kernel, sizes, (micro, cap, per_co...]
    transpose x2 -> x0, local copies, waits for them, and re-layouts: 2.77 us -> none  [the longest x1 1.47 us: shards(): small[:expert_count]]
where the time goes in v2:
time: 221 us
  Pallas kernels  219 us (99%)
    pallas_call x1, Pallas kernels, settle(): pl.pallas_call(functools.partial(settle_kernel, sizes, (micro, cap, micro...  102 us
    pallas_call x1, Pallas kernels, layer(): pl.pallas_call(functools.partial(layer_kernel, sizes, (micro, cap, per_co...  96.4 us
    pallas_call x1, Pallas kernels, finish(): pl.pallas_call(finish_kernel, out_shape=(jax.ShapeDtypeStruct((width, wid...  19.7 us

profile of v2, /device:TPU:1, one launch (start us, length us, event | category | flops | bytes accessed | tf_op | source)
XLA Modules:
  0.0 220.7 jit_solution(6438117980368485427)
XLA Ops:
  0.6 96.4 %layer.1 = (bf16[2,2,8,40,1024]{4,3,2,1,0:T(8,128)(2,1)}, bf16[2,16,40,1024]{3,2,1,0:T(8,128)(2,1)}, bf16[2,16,40,704]{3,2,1,0:T(8,128)(2,1)}, bf16[2,16,40,704]...) custom-call(bf16[128,1024]{1,0:T(8,128)(2,1)} %layer_in.3, ...), custom_call_target="tpu_custom_call" | custom-call | tf_op jit(solution)/shard_map/layer/pallas_call | solution.py:672
  97.1 102.3 %settle.1 = (bf16[128,1024]{1,0:T(8,128)(2,1)}, f32[128,1024]{1,0:T(8,128)}, bf16[4,1024,1024]{2,1,0:T(8,128)(2,1)}, f32[48,1024]{1,0:T(8,128)}) custom-call(bf16[2,2,8,40,1024]{4,3,2,1,0:T(8,128)(2,1)} %get-tuple-element.42.back_ref, s32[2,128]{1,0:T(2,128)} %bitcast.34, s32[2,128]{1,0:T(2,128)} %bitcast.36, f32[8,128]{1,0:T(8,128)} %get-tuple-element.43.gate_ref, ...), custom_call_target="tpu_custom_call" | custom-call | tf_op jit(solution)/shard_map/settle/pallas_call | solution.py:1186
  199.4 0.0 copy-start.1
  199.4 0.0 copy-start
  199.4 19.7 %finish.1 = (f32[1024,1024]{1,0:T(8,128)}, f32[1024,1024]{1,0:T(8,128)}, f32[1024,1024]{1,0:T(8,128)}, f32[1024,1024]{1,0:T(8,128)}, f32[2,704,1024]{2,1,0:T(8,1...) custom-call(f32[48,1024]{1,0:T(8,128)} %get-tuple-element.53.small, ...), custom_call_target="tpu_custom_call" | custom-call | tf_op jit(solution)/shard_map/finish/pallas_call | solution.py:788
  219.2 0.0 copy-done.1
  219.2 0.7 copy.30
  219.9 0.0 copy-done
  219.9 0.8 copy.31
Async XLA Ops:
  199.4 19.8 %copy-start.1 = (bf16[128,1024]{1,0:T(8,128)(2,1)S(1)}, bf16[128,1024]{1,0:T(8,128)(2,1)}, u32[]{:S(2)}) copy-start(bf16[128,1024]{1,0:T(8,128)(2,1)} %get-tuple-element.84) | copy-start | bytes 786436
  199.4 20.5 %copy-start = (f32[128,1024]{1,0:T(8,128)S(1)}, f32[128,1024]{1,0:T(8,128)}, u32[]{:S(2)}) copy-start(f32[128,1024]{1,0:T(8,128)} %get-tuple-element.85) | copy-start | bytes 1572868

commit v3 on v2

--- a/solution.py
+++ b/solution.py
@@ -428,16 +428,23 @@
 def layer_kernel(
     sizes, rows_per, layer_in, norm_attn, norm_moe, table_t, router_t, route_ref, slot_ref, cot_ref,
     wq_hbm, wk_hbm, wv_hbm, wo_hbm, wg_hbm, wu_hbm, wd_hbm,
-    q_out, x_hbm, hid_hbm, dg_hbm, du_hbm, gr_hbm, query, key, value, probs, context, residual, attn_in, gate_out,
-    x_ref, hid_out, dg_out, du_out, gr_out, g_ref, w_ref, weights, act, slope, away, own,
-    sem_a, sem_w, sem_e, *scratch,
+    q_out, x_hbm, hid_hbm, dg_hbm, du_hbm, gr_hbm, *attn_hbm_and_scratch,
 ):
+    attn_hbm, (gate_out, *scratch) = attn_hbm_and_scratch[:7], attn_hbm_and_scratch[7:]
+    query, key, value, probs, context, residual, attn_in = scratch[:7]
+    x_ref, hid_out, dg_out, du_out, gr_out, g_ref, w_ref, weights, act, slope, away, own = scratch[7:19]
+    sem_a, sem_w, sem_e, *scratch = scratch[19:]
     me = Place(*sizes)
     c = me.c
     seq, width = layer_in.shape
     heads, buckets = table_t.shape
     units = wg_hbm.shape[1]
     bf, f32 = jnp.bfloat16, jnp.float32
+
+    def emit(i, src, dst):
+        copy = pltpu.make_async_copy(src, dst, sem_e.at[i])
+        copy.start()
+        return copy
 
     attn_w = []
     for i, src in enumerate((wq_hbm, wk_hbm, wv_hbm, wo_hbm)):
@@ -498,6 +505,7 @@
     resid = rows + dot_as(context[...], weights[3 * width : 4 * width, :], NN)
     residual[...] = resid
     fetch = {}
+    attn_saved = (query, key, value, probs, context, residual, attn_in)
     for n, j in enumerate((c, 1 - c)):
         for i, src in enumerate((wg_hbm, wu_hbm, wd_hbm)):
             dst = weights.at[pl.ds(pl.multiple_of((2 * i + j) * units, 16), units)]
@@ -524,6 +532,7 @@
     rows_in.share("gates", gates)
     buf_x[...] = rows_in.gather(0)
     out_x.send()
+    copies = [emit(5 + i, src, dst) for i, (src, dst) in enumerate(zip(attn_saved, attn_hbm))]
     out_g.pass_on(quarter[2])
     for e, tile in enumerate(rows_in.weights()):
         buf_w[e] = tile
@@ -532,18 +541,13 @@
     out_g.cross(0)
 
     size = x_ref.shape[2]
-    step = math.gcd(column, 4)
+    step = math.gcd(column, 8)
     chunk = step * size
     back = Back(
         me, lambda i: away.at[i],
         lambda i, block: own[i, pl.ds(pl.multiple_of(block * size, 8), size), :],
         q_out, *scratch[:4], scratch[4:],
     )
-
-    def emit(i, src, dst):
-        copy = pltpu.make_async_copy(src, dst, sem_e.at[i])
-        copy.start()
-        return copy
 
     def part(i, j):
         return weights[pl.ds(pl.multiple_of((2 * i + j) * units, 16), units), :]
@@ -645,7 +649,7 @@
     back.finish(0, shares[2])
     backward(False, c, here, column)
     saved = ((x_ref, x_hbm), (hid_out, hid_hbm), (dg_out, dg_hbm), (du_out, du_hbm), (gr_out, gr_hbm))
-    copies = [emit(i, src, dst) for i, (src, dst) in enumerate(saved)]
+    copies += [emit(i, src, dst) for i, (src, dst) in enumerate(saved)]
     back.finish(0, shares[3])
     back.across(0)
     back.finish(1, back.order)
@@ -677,8 +681,15 @@
             jax.ShapeDtypeStruct((8, seq), f32),
         ),
         in_specs=[VMEM] * 8 + [any_space] * 7,
-        out_specs=(VMEM,) + (any_space,) * 5 + (VMEM,) * 8,
+        out_specs=(VMEM,) + (any_space,) * 12 + (VMEM,),
         scratch_shapes=[
+            pltpu.VMEM((seq, width), bf),
+            pltpu.VMEM((seq, width), bf),
+            pltpu.VMEM((seq, width), bf),
+            pltpu.VMEM((heads, seq, seq), f32),
+            pltpu.VMEM((seq, width), bf),
+            pltpu.VMEM((seq, width), f32),
+            pltpu.VMEM((seq, width), bf),
             pltpu.VMEM(outer.shape, bf),
             pltpu.VMEM(inner.shape, bf),
             pltpu.VMEM(inner.shape, bf),
@@ -693,7 +704,7 @@
             pltpu.VMEM((2, count * size, width), f32),
             DMA((4,)),
             DMA((2, 3)),
-            DMA((5,)),
+            DMA((12,)),
         ]
         + rows_scratch(sizes, per_core, seq, width)
         + spread_sems(sizes)
@@ -707,8 +718,8 @@
 
 def finish_kernel(small, sums_hbm, x_hbm, h_hbm, dg_hbm, du_hbm, gr_hbm, *refs):
     outs, (router_out, attn_out, moe_out, table_out) = refs[:7], refs[7:11]
-    sums, x, h, dg, du, gr, stage, sem_sum, sem_in, sem_out = refs[11:]
-    slots, rows = stage.shape[:2]
+    sums, x, h, dg, du, gr, stage, wide, sem_sum, sem_in, sem_out, sem_wide = refs[11:]
+    rows = stage.shape[1]
     width = sums.shape[1]
     units = h.shape[2]
     loads = {}
@@ -742,42 +753,41 @@
 
     jobs = []
     products = [
-        (left, right, out, j, f)
+        (left, right, out, j)
         for left, right, out in ((("dg", dg), ("x", x), 4), (("du", du), ("x", x), 5), (("h", h), ("gr", gr), 6))
         for j in range(2)
-        for f in range(0, units, rows)
     ]
     casts = list(casts)
+    every = max(1, len(casts) // len(products))
     while casts or products:
-        if casts:
-            jobs.append(casts.pop(0))
-        if products and (len(jobs) > 3 or not casts):
-            jobs.append(products.pop(0))
-    flying = [None] * slots
-    for n, job in enumerate(jobs):
-        slot = n % slots
-        if flying[slot] is not None:
-            flying[slot].wait()
-        if isinstance(job, int):
+        jobs += casts[:every]
+        casts = casts[every:]
+        jobs += products[:1]
+        products = products[1:]
+    flying = {}
+    counts = [0, 0]
+    for job in jobs:
+        product = not isinstance(job, int)
+        box, sem = (wide, sem_wide) if product else (stage, sem_out)
+        slot = counts[product] % box.shape[0]
+        counts[product] += 1
+        if (product, slot) in flying:
+            flying[product, slot].wait()
+        if product:
+            (left_key, left), (right_key, right), out, j = job
+            need((left_key, j))
+            need((right_key, j))
+            box[slot] = dot_as(left[j], right[j], TN)
+            dst = outs[out].at[j]
+        else:
             need(("sums", job))
             m, r = job * rows // width, job * rows % width
-            stage[slot] = sums[m, r : r + rows, :].astype(jnp.float32)
-            src, dst = stage.at[slot], outs[m].at[pl.ds(r, rows)]
-        else:
-            (left_key, left), (right_key, right), out, j, f = job
-            need((left_key, j))
-            need((right_key, j))
-            size = min(rows, units - f)
-            stage[slot, :size] = lax.dot_general(
-                left[j, :, f : f + size], right[j], (((0,), (0,)), ((), ())),
-                preferred_element_type=jnp.float32,
-            )
-            src, dst = stage.at[slot, pl.ds(0, size)], outs[out].at[j, pl.ds(f, size)]
-        flying[slot] = pltpu.make_async_copy(src, dst, sem_out.at[slot])
-        flying[slot].start()
-    for copy in flying:
-        if copy is not None:
-            copy.wait()
+            box[slot] = sums[m, r : r + rows, :].astype(jnp.float32)
+            dst = outs[m].at[pl.ds(r, rows)]
+        flying[product, slot] = pltpu.make_async_copy(box.at[slot], dst, sem.at[slot])
+        flying[product, slot].start()
+    for copy in flying.values():
+        copy.wait()
 
 
 def finish(sums, small, x, h, dg, du, gr, experts, table):
@@ -793,7 +803,8 @@
         in_specs=[VMEM] + [any_space] * 6,
         out_specs=(any_space,) * 7 + (VMEM,) * 4,
         scratch_shapes=[pltpu.VMEM(a.shape, a.dtype) for a in (sums, x, h, dg, du, gr)]
-        + [pltpu.VMEM((6, 256, width), f32), DMA((4 * width // 256,)), DMA((5, 2)), DMA((6,))],
+        + [pltpu.VMEM((4, 256, width), f32), pltpu.VMEM((2, units, width), f32)]
+        + [DMA((4 * width // 256,)), DMA((5, 2)), DMA((4,)), DMA((2,))],
         name="finish",
         compiler_params=pltpu.CompilerParams(vmem_limit_bytes=60 << 20),
     )(small, sums, x, h, dg, du, gr)
@@ -826,13 +837,30 @@
 
 def settle_kernel(
     sizes, rows_per, pieces,
-    back_ref, route_ref, slot_ref, gate_ref, cot_ref, layer_in, residual, context, attn_in, query, key, value, probs,
-    norm_attn, norm_moe, router_t, wq_hbm, wk_hbm, wv_hbm, wo_hbm,
+    back_hbm, route_ref, slot_ref, gate_ref, *inputs_hbm_and_rest,
+):
+    inputs_hbm, rest = inputs_hbm_and_rest[:9], inputs_hbm_and_rest[9:]
+    settle_body(sizes, rows_per, pieces, (back_hbm, *inputs_hbm), route_ref, slot_ref, gate_ref, *rest)
+
+
+def settle_body(
+    sizes, rows_per, pieces, inputs_hbm, route_ref, slot_ref, gate_ref, norm_attn, norm_moe, router_t, wq_hbm, wk_hbm, wv_hbm, wo_hbm,
     layer_out, grad_in, out_hbm, small_out,
+    back_ref, cot_ref, layer_in, residual, context, attn_in, query, key, value, probs, sem_l,
     weights, sem_a, left_ref, right_ref, small_ref, lines, out, sem_out, buf_a, buf_b, acc, *boxes,
 ):
     bf, f32 = jnp.bfloat16, jnp.float32
     micro, cap, per_core = rows_per
+    inputs = (back_ref, cot_ref, layer_in, residual, context, attn_in, query, key, value, probs)
+    loads = {}
+    for i in (5, 4, 0, 1, 3, 8, 9, 6, 7, 2):
+        loads[i] = pltpu.make_async_copy(inputs_hbm[i], inputs[i], sem_l.at[i])
+        loads[i].start()
+
+    def need(*which):
+        for i in which:
+            loads[i].wait()
+
     attn_w = []
     for i, src in ((3, wo_hbm), (0, wq_hbm), (1, wk_hbm), (2, wv_hbm)):
         attn_w.append(pltpu.make_async_copy(src, weights.at[i], sem_a.at[i]))
@@ -873,6 +901,7 @@
     def slot_b(slot):
         return buf_b.at[pl.ds(pl.multiple_of(slot * seq, seq), seq), :]
 
+    need(5, 4)
     left_ref[0] = attn_in[...]
     left_ref[1] = context[...]
     targets = [
@@ -906,6 +935,7 @@
             total = term if total is None else total + term
         return total
 
+    need(0, 1, 3)
     cot = cot_ref[...].astype(f32)
     resid = residual[...]
     chosen = [picked(low[k], 0) for k in range(2)]
@@ -946,6 +976,7 @@
     attn_w[0].wait()
     grad_context = dot_as(right_ref[3], weights[3], NT).astype(bf)
 
+    need(8, 9, 6, 7, 2)
     heads = probs.shape[0]
     pair_lanes = 2 * width // heads
     low_half = lax.broadcasted_iota(jnp.int32, (seq, pair_lanes), 1) < pair_lanes // 2
@@ -1191,9 +1222,11 @@
             jax.ShapeDtypeStruct((4, width, width), bf),
             jax.ShapeDtypeStruct((small_rows, width), f32),
         ),
-        in_specs=[VMEM] * 16 + [any_space] * 4,
+        in_specs=[any_space] + [VMEM] * 3 + [any_space] * 9 + [VMEM] * 3 + [any_space] * 4,
         out_specs=(VMEM, VMEM, any_space, VMEM),
-        scratch_shapes=[
+        scratch_shapes=[pltpu.VMEM(a.shape, a.dtype) for a in (arrays[0], *arrays[4:])]
+        + [
+            DMA((10,)),
             pltpu.VMEM((4, width, width), bf),
             DMA((4,)),
             pltpu.VMEM((2, seq, width), bf),

time: 221 us -> 214 us (0.968)
  Pallas kernels: 219 us -> 212 us
    pallas_call x1, Pallas kernels: 102 us -> 97.5 us  [settle(): pl.pallas_call(functools.partial(settle_kernel, sizes, (micro, cap, micro...]
where the time goes in v3:
time: 214 us
  Pallas kernels  212 us (99%)
    pallas_call x1, Pallas kernels, settle(): pl.pallas_call(functools.partial(settle_kernel, sizes, (micro, cap, micro...  97.5 us
    pallas_call x1, Pallas kernels, layer(): pl.pallas_call(functools.partial(layer_kernel, sizes, (micro, cap, per_co...  95.9 us
    pallas_call x1, Pallas kernels, finish(): pl.pallas_call(finish_kernel, out_shape=(jax.ShapeDtypeStruct((width, wid...  18.3 us

profile of v3, /device:TPU:1, one launch (start us, length us, event | category | flops | bytes accessed | tf_op | source)
XLA Modules:
  0.0 214.0 jit_solution(18216636056350822952)
XLA Ops:
  0.6 95.9 %layer.1 = (bf16[2,2,8,40,1024]{4,3,2,1,0:T(8,128)(2,1)}, bf16[2,16,40,1024]{3,2,1,0:T(8,128)(2,1)}, bf16[2,16,40,704]{3,2,1,0:T(8,128)(2,1)}, bf16[2,16,40,704]...) custom-call(bf16[128,1024]{1,0:T(8,128)(2,1)} %inputs_hbm_and_rest_1, ...), custom_call_target="tpu_custom_call" | custom-call | tf_op jit(solution)/shard_map/layer/pallas_call | solution.py:676
  96.6 97.5 %settle.1 = (bf16[128,1024]{1,0:T(8,128)(2,1)}, f32[128,1024]{1,0:T(8,128)}, bf16[4,1024,1024]{2,1,0:T(8,128)(2,1)}, f32[48,1024]{1,0:T(8,128)}) custom-call(bf16[2,2,8,40,1024]{4,3,2,1,0:T(8,128)(2,1)} %get-tuple-element.42.back_hbm, s32[2,128]{1,0:T(2,128)} %bitcast.34, s32[2,128]{1,0:T(2,128)} %bitcast.36, f32[8,128]{1,0:T(8,128)} %get-tuple-element.43.gate_ref, ...), custom_call_target="tpu_custom_call" | custom-call | tf_op jit(solution)/shard_map/settle/pallas_call | solution.py:1217
  194.1 0.0 copy-start.1
  194.1 0.0 copy-start
  194.1 18.3 %finish.1 = (f32[1024,1024]{1,0:T(8,128)}, f32[1024,1024]{1,0:T(8,128)}, f32[1024,1024]{1,0:T(8,128)}, f32[1024,1024]{1,0:T(8,128)}, f32[2,704,1024]{2,1,0:T(8,1...) custom-call(f32[48,1024]{1,0:T(8,128)} %get-tuple-element.53.small, ...), custom_call_target="tpu_custom_call" | custom-call | tf_op jit(solution)/shard_map/finish/pallas_call | solution.py:798
  212.5 0.0 copy-done.1
  212.5 0.7 copy.30
  213.2 0.0 copy-done
  213.2 0.8 copy.31
Async XLA Ops:
  194.1 18.4 %copy-start.1 = (bf16[128,1024]{1,0:T(8,128)(2,1)S(1)}, bf16[128,1024]{1,0:T(8,128)(2,1)}, u32[]{:S(2)}) copy-start(bf16[128,1024]{1,0:T(8,128)(2,1)} %get-tuple-element.84) | copy-start | bytes 786436
  194.1 19.1 %copy-start = (f32[128,1024]{1,0:T(8,128)S(1)}, f32[128,1024]{1,0:T(8,128)}, u32[]{:S(2)}) copy-start(f32[128,1024]{1,0:T(8,128)} %get-tuple-element.85) | copy-start | bytes 1572868

commit v4 on v3

--- a/solution.py
+++ b/solution.py
@@ -618,13 +618,13 @@
     forward(False, c, here, column)
     for i in range(3):
         fetch[1, i].wait()
-    out_x.crossed[0].wait_recv()
-    forward(True, 1 - c, here, column)
-    back.to_mate(0, 0)
     out_w.pass_column()
     out_w.cross(0)
     for s in range(1, me.ny):
         out_x.cross(s)
+    out_x.crossed[0].wait_recv()
+    forward(True, 1 - c, here, column)
+    back.to_mate(0, 0)
     for k in range(1, me.ny):
         out_x.crossed[k].wait_recv()
         forward(True, 1 - c, away_ys[k - 1], column)

time: 214 us -> 214 us (level)
  no operation moved by 1% of the time
where the time goes in v4:
time: 214 us
  Pallas kernels  212 us (99%)
    pallas_call x1, Pallas kernels, settle(): pl.pallas_call(functools.partial(settle_kernel, sizes, (micro, cap, micro...  97.6 us
    pallas_call x1, Pallas kernels, layer(): pl.pallas_call(functools.partial(layer_kernel, sizes, (micro, cap, per_co...  95.9 us
    pallas_call x1, Pallas kernels, finish(): pl.pallas_call(finish_kernel, out_shape=(jax.ShapeDtypeStruct((width, wid...  18.3 us

profile of v4, /device:TPU:1, one launch (start us, length us, event | category | flops | bytes accessed | tf_op | source)
XLA Modules:
  0.0 214.0 jit_solution(15094711961245011084)
XLA Ops:
  0.6 95.9 %layer.1 = (bf16[2,2,8,40,1024]{4,3,2,1,0:T(8,128)(2,1)}, bf16[2,16,40,1024]{3,2,1,0:T(8,128)(2,1)}, bf16[2,16,40,704]{3,2,1,0:T(8,128)(2,1)}, bf16[2,16,40,704]...) custom-call(bf16[128,1024]{1,0:T(8,128)(2,1)} %inputs_hbm_and_rest_1, ...), custom_call_target="tpu_custom_call" | custom-call | tf_op jit(solution)/shard_map/layer/pallas_call | solution.py:676
  96.6 97.6 %settle.1 = (bf16[128,1024]{1,0:T(8,128)(2,1)}, f32[128,1024]{1,0:T(8,128)}, bf16[4,1024,1024]{2,1,0:T(8,128)(2,1)}, f32[48,1024]{1,0:T(8,128)}) custom-call(bf16[2,2,8,40,1024]{4,3,2,1,0:T(8,128)(2,1)} %get-tuple-element.42.back_hbm, s32[2,128]{1,0:T(2,128)} %bitcast.34, s32[2,128]{1,0:T(2,128)} %bitcast.36, f32[8,128]{1,0:T(8,128)} %get-tuple-element.43.gate_ref, ...), custom_call_target="tpu_custom_call" | custom-call | tf_op jit(solution)/shard_map/settle/pallas_call | solution.py:1217
  194.1 0.0 copy-start.1
  194.1 0.0 copy-start
  194.1 18.3 %finish.1 = (f32[1024,1024]{1,0:T(8,128)}, f32[1024,1024]{1,0:T(8,128)}, f32[1024,1024]{1,0:T(8,128)}, f32[1024,1024]{1,0:T(8,128)}, f32[2,704,1024]{2,1,0:T(8,1...) custom-call(f32[48,1024]{1,0:T(8,128)} %get-tuple-element.53.small, ...), custom_call_target="tpu_custom_call" | custom-call | tf_op jit(solution)/shard_map/finish/pallas_call | solution.py:798
  212.5 0.0 copy-done.1
  212.5 0.7 copy.30
  213.2 0.0 copy-done
  213.2 0.8 copy.31
Async XLA Ops:
  194.1 18.4 %copy-start.1 = (bf16[128,1024]{1,0:T(8,128)(2,1)S(1)}, bf16[128,1024]{1,0:T(8,128)(2,1)}, u32[]{:S(2)}) copy-start(bf16[128,1024]{1,0:T(8,128)(2,1)} %get-tuple-element.84) | copy-start | bytes 786436
  194.1 19.1 %copy-start = (f32[128,1024]{1,0:T(8,128)S(1)}, f32[128,1024]{1,0:T(8,128)}, u32[]{:S(2)}) copy-start(f32[128,1024]{1,0:T(8,128)} %get-tuple-element.85) | copy-start | bytes 1572868
